TPU v7x, 32 devices: a whole 2x2x4 slice. The times are simulated.
32 devices in a mesh: row: 16 (over z, y, core), col: 2 (over x).
Axes of the slice: x: 2, y: 2, z: 4, core: 2. Of those that a mesh axis runs over, the one named last changes fastest.
Arguments:
- c_matrix: bfloat16 [2, 3072, 6144], P(None, 'row', 'col'), may hold values from -6 to 6
- beta_values: bfloat16 [1, 48, 6, 128, 128], P(None, 'col'), may hold values from -0.21875 to 0.21875
- beta_rows: int32 [1, 48, 6], P(None, 'col'), may hold values from 0 to 47, as said below
- alpha_values: bfloat16 [1, 2, 16, 4, 192, 192], P(None, None, 'row'), may hold values from -0.21875 to 0.21875
- alpha_rows: int32 [1, 2, 16, 4], P(None, None, 'row'), may hold values from 0 to 31, as said below
- gaps: float32 [2, 3072, 6144], P(None, 'row', 'col'), may hold values from 0.5 to 4
Outputs:
- update: float32 [2, 3072, 6144], P(None, 'row', 'col')
Inputs may be any that keep to these rules, and one draw needn't show every extreme that they name: For every k and tile column j, beta_rows[k, j] lists 6 distinct tile rows and its first entry is j. For every k, g, r, alpha_rows[k, g, r] lists 4 distinct tile rows and its first entry is the tile column g * 16 + r.
All inputs are finite; a program needn't handle non-finite values.
Results may differ from a plain program's by a relative error of at most 0.0029.
Values may be sent and summed in bfloat16 or wider, within the bound.
A program may use at most 192 MiB of HBM per device.

v0:
```python
import functools

import jax
import jax.numpy as jnp
from jax import lax
from jax.experimental import pallas as pl
from jax.experimental.pallas import tpu as pltpu
from jax.sharding import PartitionSpec as P

CONTRACT_LAST = (((1,), (1,)), ((), ()))


def beta_kernel(listed, held, rows_ref, c_ref, b_ref, xt_ref):
    k, j = pl.program_id(0), pl.program_id(1)
    width = b_ref.shape[-1]
    picked = []
    for z in range(listed):
        tile = rows_ref[k, j, z]
        owner = tile // held
        start = pl.multiple_of((tile - owner * held) * width, width)
        picked.append(c_ref[owner, :, pl.ds(start, width)])
    lhs = b_ref[0, 0].reshape(listed * width, width)
    product = lax.dot_general(
        lhs, jnp.concatenate(picked, axis=1), (((0,), (1,)), ((), ())),
        preferred_element_type=jnp.float32,
    )
    xt_ref[0] = product.astype(xt_ref.dtype)


def beta_products(gathered, beta_values, beta_rows):
    pairs, tiles, listed, width, _ = beta_values.shape
    owners, rows, columns = gathered.shape
    return pl.pallas_call(
        functools.partial(beta_kernel, listed, columns // width),
        grid_spec=pltpu.PrefetchScalarGridSpec(
            num_scalar_prefetch=1,
            grid=(pairs, tiles),
            in_specs=[
                pl.BlockSpec((owners, rows, columns), lambda k, j, s: (0, 0, 0)),
                pl.BlockSpec((1, 1, listed, width, width), lambda k, j, s: (k, j, 0, 0, 0)),
            ],
            out_specs=pl.BlockSpec((1, width, rows), lambda k, j, s: (k, j, 0)),
        ),
        out_shape=jax.ShapeDtypeStruct((pairs, tiles * width, rows), jnp.bfloat16),
        compiler_params=pltpu.CompilerParams(vmem_limit_bytes=56 << 20),
        name="beta_products",
    )(beta_rows, gathered, beta_values)


def pack_alpha(flat_ref, packed_ref):
    size, tile = flat_ref.shape
    half, whole = size // 2, tile // 128
    for i in range(whole):
        packed_ref[pl.ds(i * size, size), :] = flat_ref[:, i * 128 : (i + 1) * 128]
    packed_ref[pl.ds(whole * size, half), :] = jnp.concatenate(
        [flat_ref[pl.ds(0, half), whole * 128 :], flat_ref[pl.ds(half, half), whole * 128 :]], axis=1
    )


def packed_product(a_ref, at, slot, slots, listed, tile, x):
    size, whole = listed * tile, tile // 128
    parts = [a_ref[at, pl.ds(i * slots * size + slot * size, size), :] for i in range(whole)]
    parts.append(a_ref[at, pl.ds(whole * slots * size + slot % (slots // 2) * size, size), :])
    blank = jnp.zeros((x.shape[0], 64), x.dtype)
    tail = [x[:, whole * 128 :], blank]
    if slot >= slots // 2:
        tail = tail[::-1]
    wide = jnp.concatenate([x[:, : whole * 128]] + tail, axis=1)
    return lax.dot_general(
        jnp.concatenate(parts, axis=1), wide, CONTRACT_LAST, preferred_element_type=jnp.float32
    )


def alpha_kernel(groups, rows_ref, a_ref, x_ref, own_ref, mirror_ref, acc_ref):
    r = pl.program_id(0)
    row_devices = pl.num_programs(0)
    pairs = x_ref.shape[2]
    listed, tile = rows_ref.shape[2], acc_ref.shape[1]

    @pl.when(r == 0)
    def _():
        acc_ref[...] = jnp.zeros_like(acc_ref)

    for i in range(x_ref.shape[1]):
        at = r * x_ref.shape[1] + i
        for k in range(pairs):
            parts = [x_ref[c, i, k] for c in range(x_ref.shape[0])]
            merged = jnp.concatenate(parts, axis=1) if len(parts) > 1 else parts[0]
            for g in range(groups):
                x = merged[:, g * tile : (g + 1) * tile]
                slot = k * groups + g
                if len(a_ref.shape) == 3:
                    product = packed_product(a_ref, i, slot, pairs * groups, listed, tile, x)
                    for z in range(listed):
                        acc_ref[rows_ref[at, slot, z]] += product[z * tile : (z + 1) * tile]
                else:

                    @pl.loop(0, listed)
                    def _(z):
                        acc_ref[rows_ref[at, slot, z]] += lax.dot_general(
                            a_ref[i, slot, z], x, CONTRACT_LAST,
                            preferred_element_type=jnp.float32,
                        )

    @pl.when(r == row_devices - 1)
    def _():
        count = acc_ref.shape[0] // groups
        for g in range(groups):
            for to in range(count):
                turned = acc_ref[g * count + to].astype(own_ref.dtype).T
                own_ref[to, :, g * tile : (g + 1) * tile] = turned
                mirror_ref[g, :, to * tile : (to + 1) * tile] = turned


def alpha_products(alpha_all, rows_all, x_strip, groups):
    row_devices, rest = alpha_all.shape[0], alpha_all.shape[1:]
    tile = x_strip.shape[0] * x_strip.shape[-1] // groups
    per = 4 if len(rest) == 2 and row_devices % 4 == 0 else 1
    chunks, _, pairs, strip, chunk = x_strip.shape
    return pl.pallas_call(
        functools.partial(alpha_kernel, groups),
        grid_spec=pltpu.PrefetchScalarGridSpec(
            num_scalar_prefetch=1,
            grid=(row_devices // per,),
            in_specs=[
                pl.BlockSpec((per,) + rest, lambda r, s: (r,) + (0,) * len(rest)),
                pl.BlockSpec((chunks, per, pairs, strip, chunk), lambda r, s: (0, r, 0, 0, 0)),
            ],
            out_specs=[
                pl.BlockSpec((row_devices, strip, groups * tile), lambda r, s: (0, 0, 0)),
                pl.BlockSpec((groups, strip, row_devices * tile), lambda r, s: (0, 0, 0)),
            ],
            scratch_shapes=[pltpu.VMEM((groups * row_devices, tile, strip), jnp.float32)],
        ),
        out_shape=[
            jax.ShapeDtypeStruct((row_devices, strip, groups * tile), jnp.bfloat16),
            jax.ShapeDtypeStruct((groups, strip, row_devices * tile), jnp.bfloat16),
        ],
        compiler_params=pltpu.CompilerParams(vmem_limit_bytes=56 << 20),
        name="alpha_products",
    )(rows_all, alpha_all, x_strip)


def final_kernel(own_ref, mirror_ref, gaps_ref, out_ref):
    own = own_ref[...].T.astype(jnp.float32)
    out_ref[...] = (own + mirror_ref[...].astype(jnp.float32)) / gaps_ref[...]


def final(own, mirror, gaps):
    rows, columns = gaps.shape
    block = next(n for n in (384, 256, 128) if columns % n == 0)
    wide = pl.BlockSpec((rows, block), lambda i: (0, i))
    return pl.pallas_call(
        final_kernel,
        grid=(columns // block,),
        in_specs=[pl.BlockSpec((block, rows), lambda i: (i, 0)), wide, wide],
        out_specs=wide,
        out_shape=jax.ShapeDtypeStruct((rows, columns), jnp.float32),
        name="final",
    )(own, mirror, gaps)


def greet(axes):
    barrier = pltpu.get_barrier_semaphore()
    total = 0
    for axis in axes:
        size, me = lax.axis_size(axis), lax.axis_index(axis)
        total += size - 1

        @pl.loop(1, size)
        def _(off):
            pl.semaphore_signal(
                barrier, inc=1, device_id={axis: lax.rem(me + off, size)},
                device_id_type=pl.DeviceIdType.MESH,
            )

    pl.semaphore_wait(barrier, total)


def alternate(step, size):
    odd = lax.rem(step, 2)
    return odd * ((step + 1) // 2) + (1 - odd) * (size - step // 2)


def remote(src, dst, send_sem, recv_sem, axis, peer):
    return pltpu.make_async_remote_copy(
        src_ref=src, dst_ref=dst, send_sem=send_sem, recv_sem=recv_sem,
        device_id={axis: peer}, device_id_type=pl.DeviceIdType.MESH,
    )


def spread_kernel(chunks, rows_ref, c_ref, b_ref, list_ref, flat_ref, x_ref, lists_ref, all_ref, *scratch):
    held, sent = scratch[:chunks], scratch[chunks : 2 * chunks]
    (local_sem, c_send, c_recv, x_send, x_recv, own_sem, l_send, l_recv, l_own, up_send, up_recv,
     down_send, down_recv, y_send, y_recv, core_send, core_recv, a_own, a_ref) = scratch[2 * chunks :]
    row_devices, row = lax.axis_size("row"), lax.axis_index("row")
    col_devices, col = lax.axis_size("col"), lax.axis_index("col")
    pairs, tiles, listed, width, _ = b_ref.shape
    rows, columns = c_ref.shape
    per_owner = columns // width
    chunk = rows // chunks
    strip = per_owner * width // row_devices

    def own_c(c, t):
        return pltpu.make_async_copy(
            c_ref.at[pl.ds(c * chunk, chunk), pl.ds(pl.multiple_of(t * width, width), width)],
            held[c].at[col * per_owner + t], local_sem.at[c, t],
        )

    def send_c(c, off, t):
        return remote(
            c_ref.at[pl.ds(c * chunk, chunk), pl.ds(pl.multiple_of(t * width, width), width)],
            held[c].at[col * per_owner + t], c_send.at[c, off - 1, t], c_recv.at[c, off - 1, t],
            "col", lax.rem(col + off, col_devices),
        )

    def send_x(c, off):
        peer = lax.rem(row + off, row_devices)
        start = pl.multiple_of(peer * strip, 16)
        return remote(
            sent[c].at[:, pl.ds(start, strip), :], x_ref.at[c, row], x_send.at[c, off - 1],
            x_recv.at[c, off - 1], "row", peer,
        )

    def own_x(c):
        start = pl.multiple_of(row * strip, 16)
        return pltpu.make_async_copy(
            sent[c].at[:, pl.ds(start, strip), :], x_ref.at[c, row], own_sem.at[c]
        )

    def send_list(off):
        return remote(
            list_ref, lists_ref.at[row], l_send.at[off - 1], l_recv.at[off - 1], "row",
            lax.rem(row + off, row_devices),
        )

    lines = row_devices // 4
    z, y, core = row // 4, lax.rem(row // 2, 2), lax.rem(row, 2)

    def block(at_z, at_y, at_core):
        return (at_z * 2 + at_y) * 2 + at_core

    def hand(source, at, send_sem, recv_sem, peer):
        return remote(source, all_ref.at[at], send_sem, recv_sem, "row", peer)

    def up(step, first=False):
        at = block(z - step, y, core)
        source = a_ref if first else all_ref.at[at]
        return hand(source, at, up_send.at[step], up_recv.at[step], block(z + 1, y, core))

    def down(step, first=False):
        at = block(z + step, y, core)
        source = a_ref if first else all_ref.at[at]
        return hand(source, at, down_send.at[step], down_recv.at[step], block(z - 1, y, core))

    def over_y(at_z, first=False):
        at = block(at_z, y, core)
        source = a_ref if first else all_ref.at[at]
        return hand(source, at, y_send.at[at_z], y_recv.at[at_z], block(z, 1 - y, core))

    def over_core(at_z, at_y, first=False):
        at = block(at_z, at_y, core)
        source = a_ref if first else all_ref.at[at]
        sem = at_z * 2 + at_y
        return hand(source, at, core_send.at[sem], core_recv.at[sem], block(z, y, 1 - core))

    def arrived(at, recv_sem, send_sem):
        hand(all_ref.at[at], at, send_sem, recv_sem, block(z, y, 1 - core)).wait_recv()

    def relay(step):
        @pl.when(z - 1 - step >= 0)
        def _():
            arrived(block(z - 1 - step, y, core), up_recv.at[step], up_send.at[step])
            if step + 1 < lines - 1:

                @pl.when(z + 1 < lines)
                def _():
                    up(step + 1).start()

            over_y(z - 1 - step).start()
            over_core(z - 1 - step, y).start()

        @pl.when(z + 1 + step < lines)
        def _():
            arrived(block(z + 1 + step, y, core), down_recv.at[step], down_send.at[step])
            if step + 1 < lines - 1:

                @pl.when(z >= 1)
                def _():
                    down(step + 1).start()

            over_y(z + 1 + step).start()
            over_core(z + 1 + step, y).start()

    def cross(step):
        at_z = lax.rem(z + step, lines)
        arrived(block(at_z, 1 - y, core), y_recv.at[at_z], y_send.at[at_z])
        over_core(at_z, 1 - y).start()

    own_a = pltpu.make_async_copy(a_ref, all_ref.at[row], a_own)
    own_list = pltpu.make_async_copy(list_ref, lists_ref.at[row], l_own)
    for c in range(chunks):

        @pl.loop(0, per_owner)
        def _(t):
            own_c(c, t).start()

    own_list.start()
    pack_alpha(flat_ref, a_ref)
    greet(("row", "col"))
    for c in range(chunks):
        for off in range(1, col_devices):

            @pl.loop(0, per_owner)
            def _(t):
                send_c(c, off, t).start()

    @pl.when(z + 1 < lines)
    def _():
        up(0, True).start()

    @pl.when(z >= 1)
    def _():
        down(0, True).start()

    over_y(z, True).start()
    over_core(z, y, True).start()
    own_a.start()

    @pl.loop(1, row_devices)
    def _(off):
        send_list(off).start()

    relayed = 0
    for c in range(chunks):
        if relayed < lines - 1:
            relay(relayed)
            relayed += 1

        @pl.loop(0, per_owner)
        def _(t):
            own_c(c, t).wait()
            for off in range(1, col_devices):
                send_c(c, off, t).wait_recv()

        @pl.loop(0, tiles)
        def _(j):
            for k in range(pairs):
                picked = [held[c][rows_ref[k, j, z]] for z in range(listed)]
                product = lax.dot_general(
                    b_ref[k, j].reshape(listed * width, width), jnp.concatenate(picked, axis=1),
                    (((0,), (1,)), ((), ())), preferred_element_type=jnp.float32,
                )
                sent[c][k, pl.ds(pl.multiple_of(j * width, width), width), :] = product.astype(
                    jnp.bfloat16
                )

        @pl.loop(1, row_devices)
        def _(off):
            send_x(c, alternate(off, row_devices)).start()

        own_x(c).start()
        if c == 0:
            cross(0)

    for step in range(relayed, lines - 1):
        relay(step)
    for step in range(1, lines):
        cross(step)
    own_a.wait()
    for step in range(lines - 1):

        @pl.when((z - step >= 0) & (z + 1 < lines))
        def _():
            up(step, step == 0).wait_send()

        @pl.when((z + step < lines) & (z >= 1))
        def _():
            down(step, step == 0).wait_send()

    for at_z in range(lines):
        over_y(at_z).wait_send()
        for at_y in range(2):
            over_core(at_z, at_y).wait_send()
            sem = at_z * 2 + at_y
            arrived(block(at_z, at_y, 1 - core), core_recv.at[sem], core_send.at[sem])
    own_list.wait()

    @pl.loop(1, row_devices)
    def _(off):
        send_list(off).wait()

    for c in range(chunks):
        own_x(c).wait()
        for off in range(1, col_devices):

            @pl.loop(0, per_owner)
            def _(t):
                send_c(c, off, t).wait_send()

        @pl.loop(1, row_devices)
        def _(off):
            send_x(c, off).wait()


def spread(c_matrix, beta_values, beta_rows, alpha_list, flat, row_devices, col_devices, chunk):
    rows, columns = c_matrix.shape
    pairs, _, _, width, _ = beta_values.shape
    packed_shape = (flat.shape[0] * flat.shape[1] // 128, 128)
    held = columns // width
    strip, chunks = columns // row_devices, rows // chunk
    dma = pltpu.SemaphoreType.DMA
    anywhere = pl.BlockSpec(memory_space=pl.ANY)
    return pl.pallas_call(
        functools.partial(spread_kernel, chunks),
        in_specs=[
            pl.BlockSpec(memory_space=pltpu.SMEM), anywhere,
            pl.BlockSpec(memory_space=pltpu.VMEM), pl.BlockSpec(memory_space=pltpu.VMEM),
            pl.BlockSpec(memory_space=pltpu.VMEM),
        ],
        out_specs=[anywhere, anywhere, anywhere],
        out_shape=[
            jax.ShapeDtypeStruct((chunks, row_devices, pairs, strip, chunk), jnp.bfloat16),
            jax.ShapeDtypeStruct((row_devices,) + alpha_list.shape, jnp.int32),
            jax.ShapeDtypeStruct((row_devices,) + packed_shape, flat.dtype),
        ],
        scratch_shapes=[pltpu.VMEM((col_devices * columns // width, chunk, width), jnp.bfloat16)] * chunks
        + [pltpu.VMEM((pairs, columns, chunk), jnp.bfloat16)] * chunks
        + [
            dma((chunks, held)), dma((chunks, col_devices - 1, held)),
            dma((chunks, col_devices - 1, held)),
            dma((chunks, row_devices - 1)), dma((chunks, row_devices - 1)), dma((chunks,)),
            dma((row_devices - 1,)), dma((row_devices - 1,)), dma,
        ]
        + [dma((row_devices // 4 - 1,))] * 4
        + [dma((row_devices // 4,))] * 2
        + [dma((row_devices // 2,))] * 2
        + [dma, pltpu.VMEM(packed_shape, flat.dtype)],
        compiler_params=pltpu.CompilerParams(
            collective_id=0, has_side_effects=True, vmem_limit_bytes=56 << 20
        ),
        cost_estimate=pl.CostEstimate(
            flops=1 << 37, bytes_accessed=1 << 28, transcendentals=0
        ),
        name="spread",
    )(beta_rows, c_matrix, beta_values, alpha_list, flat)


def exchange_kernel(own_ref, mirror_ref, own_out, mirror_out, o_send, o_recv, m_send, m_recv, sems):
    row_devices, row = lax.axis_size("row"), lax.axis_index("row")
    col_devices, col = lax.axis_size("col"), lax.axis_index("col")

    def send_own(off):
        peer = lax.rem(row + off, row_devices)
        return remote(
            own_ref.at[peer], own_out.at[row], o_send.at[off - 1], o_recv.at[off - 1], "row", peer
        )

    def send_mirror(off):
        peer = lax.rem(col + off, col_devices)
        return remote(
            mirror_ref.at[peer], mirror_out.at[col], m_send.at[off - 1], m_recv.at[off - 1],
            "col", peer,
        )

    stay_own = pltpu.make_async_copy(own_ref.at[row], own_out.at[row], sems.at[0])
    stay_mirror = pltpu.make_async_copy(mirror_ref.at[col], mirror_out.at[col], sems.at[1])
    greet(("row", "col"))

    @pl.loop(1, col_devices)
    def _(off):
        send_mirror(off).start()

    @pl.loop(1, row_devices)
    def _(off):
        send_own(alternate(off, row_devices)).start()

    stay_own.start()
    stay_mirror.start()
    stay_own.wait()
    stay_mirror.wait()

    @pl.loop(1, row_devices)
    def _(off):
        send_own(off).wait()

    @pl.loop(1, col_devices)
    def _(off):
        send_mirror(off).wait()


def exchange(own, mirror):
    dma = pltpu.SemaphoreType.DMA
    anywhere = pl.BlockSpec(memory_space=pl.ANY)
    local = pl.BlockSpec(memory_space=pltpu.VMEM)
    row_devices, col_devices = own.shape[0], mirror.shape[0]
    return pl.pallas_call(
        exchange_kernel,
        in_specs=[local, local],
        out_specs=[anywhere, anywhere],
        out_shape=[
            jax.ShapeDtypeStruct(own.shape, own.dtype),
            jax.ShapeDtypeStruct(mirror.shape, mirror.dtype),
        ],
        scratch_shapes=[
            dma((row_devices - 1,)), dma((row_devices - 1,)),
            dma((col_devices - 1,)), dma((col_devices - 1,)), dma((2,)),
        ],
        compiler_params=pltpu.CompilerParams(
            collective_id=1, has_side_effects=True, vmem_limit_bytes=56 << 20
        ),
        name="exchange",
    )(own, mirror)


def per_device(c_matrix, beta_values, beta_rows, alpha_values, alpha_rows, gaps):
    row_devices, col_devices = lax.axis_size("row"), lax.axis_size("col")
    groups, stretch, columns = c_matrix.shape
    pairs, _, _, listed, tile, _ = alpha_values.shape
    rows, chunk = groups * stretch, beta_values.shape[-1]
    c_rows = c_matrix.reshape(rows, columns)
    alpha_tiles = alpha_values.reshape(pairs * groups, listed, tile, tile)
    alpha_list = alpha_rows.reshape(pairs * groups, listed)
    own_kernels = stretch % 16 == 0 and rows % chunk == 0 and tile % 128 == 64
    own_kernels = own_kernels and row_devices % 4 == 0 and pairs * groups % 2 == 0
    if own_kernels:
        entries = alpha_list.size
        padded = jnp.pad(alpha_list.reshape(-1), (0, -entries % 1024)).reshape(-1, 128)
        x_strip, rows_all, alpha_all = spread(
            c_rows, beta_values, beta_rows, padded, alpha_tiles.reshape(-1, tile), row_devices,
            col_devices, chunk,
        )
        rows_all = rows_all.reshape(row_devices, -1)[:, :entries]
        rows_all = rows_all.reshape(row_devices, pairs * groups, listed)
    else:
        rows_all = lax.all_gather(alpha_list, "row")
        alpha_all = lax.all_gather(alpha_tiles, "row")
        xt = beta_products(lax.all_gather(c_rows, "col"), beta_values, beta_rows)
        xt = jnp.moveaxis(xt.reshape(pairs, row_devices, stretch, rows), 1, 0)
        x_strip = lax.all_to_all(xt, "row", 0, 0)[None]
    own, mirror = alpha_products(alpha_all, rows_all, x_strip, groups)
    if own_kernels:
        own, mirror = exchange(own, mirror)
    else:
        own = lax.all_to_all(own, "row", 0, 0)
        mirror = lax.all_to_all(mirror, "col", 0, 0)
    out = final(
        own.reshape(columns, groups * stretch),
        mirror.reshape(groups * stretch, columns),
        gaps.reshape(groups * stretch, columns),
    )
    return out.reshape(gaps.shape)


def solution(mesh):
    placed = (
        P(None, "row", "col"),
        P(None, "col", None, None, None),
        P(None, "col", None),
        P(None, None, "row", None, None, None),
        P(None, None, "row", None),
        P(None, "row", "col"),
    )
    return jax.shard_map(
        per_device, mesh=mesh, in_specs=placed, out_specs=P(None, "row", "col"), check_vma=False
    )
```

profile of v0, /device:TPU:0, one launch (start us, length us, event | category | flops | bytes accessed | tf_op | source)
XLA Modules:
  0.0 184.2 jit_solution(16022220115843045673)
XLA Ops:
  0.0 0.5 broadcast.5
  0.5 1.3 reduce.3
  1.9 0.1 reshape_reshape.6
  1.9 0.6 pad_bitcast_fusion.list_ref
  2.5 1.4 copy.7.rows_ref
  3.9 98.6 %spread.1 = (bf16[3,16,1,192,128]{4,3,2,1,0:T(8,128)(2,1)}, s32[16,8,128]{2,1,0:T(8,128)}, bf16[16,2304,128]{2,1,0:T(8,128)(2,1)}) custom-call(s32[1,24,6]{2,1,0:T(8,128)} %copy.7.rows_ref, bf16[384,3072]{1,0:T(8,128)(2,1)} %bitcast.15, bf16[1,24,6,128,128]{4,3,2,1,0:T(8,128)(2,1)} %b_ref.1, s32[8,128]{1,0:T(8,128)} %pad_bitcast_fusion.list_ref, ...), custom_call_target="tpu_custom_call" | custom-call | flops 137438953472 | bytes 268435456 | tf_op jit(solution)/shard_map/spread/pallas_call | solution.py:414
  102.5 1.0 copy.10
  103.5 0.7 copy.9.rows_ref
  104.2 12.5 %alpha_products.1 = (bf16[16,192,384]{2,1,0:T(8,128)(2,1)}, bf16[2,192,3072]{2,1,0:T(8,128)(2,1)}) custom-call(s32[16,2,4]{2,1,0:T(2,128)} %copy.9.rows_ref, bf16[16,2304,128]{2,1,0:T(8,128)(2,1)} %get-tuple-element.13.a_ref, bf16[3,16,1,192,128]{4,3,2,1,0:T(8,128)(2,1)} %get-tuple-element.14.x_ref), custom_call_target="tpu_custom_call" | custom-call | tf_op jit(solution)/shard_map/alpha_products/pallas_call | solution.py:120
  116.7 59.2 %exchange.1 = (bf16[16,192,384]{2,1,0:T(8,128)(2,1)}, bf16[2,192,3072]{2,1,0:T(8,128)(2,1)}) custom-call(bf16[16,192,384]{2,1,0:T(8,128)(2,1)} %get-tuple-element.15.own_ref, bf16[2,192,3072]{2,1,0:T(8,128)(2,1)} %get-tuple-element.16.mirror_ref), custom_call_target="tpu_custom_call" | custom-call | tf_op jit(solution)/shard_map/exchange/pallas_call | solution.py:497
  175.9 8.3 %final.1 = f32[384,3072]{1,0:T(8,128)} custom-call(bf16[3072,384]{1,0:T(8,128)(2,1)} %bitcast.11, bf16[384,3072]{1,0:T(8,128)(2,1)} %bitcast.12, f32[384,3072]{1,0:T(8,128)} %bitcast.10), custom_call_target="tpu_custom_call" | custom-call | tf_op jit(solution)/shard_map/final/pallas_call | solution.py:153
  (1 shorter events, 0.0 us)
where the time goes:
time: 185 us; the launch traced here: 184 us
  Pallas kernels  179 us (97%)
  local copies, waits for them, and re-layouts  4.28 us (2%)
    pallas_call x1, Pallas kernels, spread(): pl.pallas_call(functools.partial(spread_kernel, chunks), in_specs=[pl.Blo...  98.6 us
    pallas_call x1, Pallas kernels, exchange(): pl.pallas_call(exchange_kernel, in_specs=[local, local], out_specs=[anywh...  59.2 us
    pallas_call x1, Pallas kernels, alpha_products(): pl.pallas_call(functools.partial(alpha_kernel, groups), grid_spec=pltpu.P...  12.5 us
    pallas_call x1, Pallas kernels, final(): pl.pallas_call(final_kernel, grid=(columns // block,), in_specs=[pl.Block...  8.27 us

commit v1 on v0

v1 whole, which is shorter than its diff:
```python
import functools

import jax
import jax.numpy as jnp
from jax import lax
from jax.experimental import pallas as pl
from jax.experimental.pallas import tpu as pltpu
from jax.sharding import PartitionSpec as P

CONTRACT_LAST = (((1,), (1,)), ((), ()))


def beta_kernel(listed, held, rows_ref, c_ref, b_ref, xt_ref):
    k, j = pl.program_id(0), pl.program_id(1)
    width = b_ref.shape[-1]
    picked = []
    for z in range(listed):
        tile = rows_ref[k, j, z]
        owner = tile // held
        start = pl.multiple_of((tile - owner * held) * width, width)
        picked.append(c_ref[owner, :, pl.ds(start, width)])
    lhs = b_ref[0, 0].reshape(listed * width, width)
    product = lax.dot_general(
        lhs, jnp.concatenate(picked, axis=1), (((0,), (1,)), ((), ())),
        preferred_element_type=jnp.float32,
    )
    xt_ref[0] = product.astype(xt_ref.dtype)


def beta_products(gathered, beta_values, beta_rows):
    pairs, tiles, listed, width, _ = beta_values.shape
    owners, rows, columns = gathered.shape
    return pl.pallas_call(
        functools.partial(beta_kernel, listed, columns // width),
        grid_spec=pltpu.PrefetchScalarGridSpec(
            num_scalar_prefetch=1,
            grid=(pairs, tiles),
            in_specs=[
                pl.BlockSpec((owners, rows, columns), lambda k, j, s: (0, 0, 0)),
                pl.BlockSpec((1, 1, listed, width, width), lambda k, j, s: (k, j, 0, 0, 0)),
            ],
            out_specs=pl.BlockSpec((1, width, rows), lambda k, j, s: (k, j, 0)),
        ),
        out_shape=jax.ShapeDtypeStruct((pairs, tiles * width, rows), jnp.bfloat16),
        compiler_params=pltpu.CompilerParams(vmem_limit_bytes=56 << 20),
        name="beta_products",
    )(beta_rows, gathered, beta_values)


def alpha_kernel(groups, rows_ref, a_ref, x_ref, own_ref, mirror_ref, acc_ref):
    r = pl.program_id(0)
    row_devices = pl.num_programs(0)
    pairs = x_ref.shape[2]
    listed, tile = rows_ref.shape[2], acc_ref.shape[1]

    @pl.when(r == 0)
    def _():
        acc_ref[...] = jnp.zeros_like(acc_ref)

    for i in range(x_ref.shape[1]):
        at = r * x_ref.shape[1] + i
        for k in range(pairs):
            parts = [x_ref[c, i, k] for c in range(x_ref.shape[0])]
            merged = jnp.concatenate(parts, axis=1) if len(parts) > 1 else parts[0]
            for g in range(groups):
                x = merged[:, g * tile : (g + 1) * tile]
                slot = k * groups + g

                @pl.loop(0, listed)
                def _(z):
                    acc_ref[rows_ref[at, slot, z]] += lax.dot_general(
                        a_ref[i, slot, z], x, CONTRACT_LAST, preferred_element_type=jnp.float32
                    )

    @pl.when(r == row_devices - 1)
    def _():
        count = acc_ref.shape[0] // groups
        for g in range(groups):
            for to in range(count):
                turned = acc_ref[g * count + to].astype(own_ref.dtype).T
                own_ref[to, :, g * tile : (g + 1) * tile] = turned
                mirror_ref[g, :, to * tile : (to + 1) * tile] = turned


def alpha_products(alpha_all, rows_all, x_strip, groups):
    row_devices, rest = alpha_all.shape[0], alpha_all.shape[1:]
    tile = x_strip.shape[0] * x_strip.shape[-1] // groups
    per = 1
    chunks, _, pairs, strip, chunk = x_strip.shape
    return pl.pallas_call(
        functools.partial(alpha_kernel, groups),
        grid_spec=pltpu.PrefetchScalarGridSpec(
            num_scalar_prefetch=1,
            grid=(row_devices // per,),
            in_specs=[
                pl.BlockSpec((per,) + rest, lambda r, s: (r,) + (0,) * len(rest)),
                pl.BlockSpec((chunks, per, pairs, strip, chunk), lambda r, s: (0, r, 0, 0, 0)),
            ],
            out_specs=[
                pl.BlockSpec((row_devices, strip, groups * tile), lambda r, s: (0, 0, 0)),
                pl.BlockSpec((groups, strip, row_devices * tile), lambda r, s: (0, 0, 0)),
            ],
            scratch_shapes=[pltpu.VMEM((groups * row_devices, tile, strip), jnp.float32)],
        ),
        out_shape=[
            jax.ShapeDtypeStruct((row_devices, strip, groups * tile), jnp.bfloat16),
            jax.ShapeDtypeStruct((groups, strip, row_devices * tile), jnp.bfloat16),
        ],
        compiler_params=pltpu.CompilerParams(vmem_limit_bytes=56 << 20),
        name="alpha_products",
    )(rows_all, alpha_all, x_strip)


def final_kernel(own_ref, mirror_ref, gaps_ref, out_ref):
    own = own_ref[...].T.astype(jnp.float32)
    out_ref[...] = (own + mirror_ref[...].astype(jnp.float32)) / gaps_ref[...]


def final(own, mirror, gaps):
    rows, columns = gaps.shape
    block = next(n for n in (384, 256, 128) if columns % n == 0)
    wide = pl.BlockSpec((rows, block), lambda i: (0, i))
    return pl.pallas_call(
        final_kernel,
        grid=(columns // block,),
        in_specs=[pl.BlockSpec((block, rows), lambda i: (i, 0)), wide, wide],
        out_specs=wide,
        out_shape=jax.ShapeDtypeStruct((rows, columns), jnp.float32),
        name="final",
    )(own, mirror, gaps)


def greet(axes):
    barrier = pltpu.get_barrier_semaphore()
    total = 0
    for axis in axes:
        size, me = lax.axis_size(axis), lax.axis_index(axis)
        total += size - 1

        @pl.loop(1, size)
        def _(off):
            pl.semaphore_signal(
                barrier, inc=1, device_id={axis: lax.rem(me + off, size)},
                device_id_type=pl.DeviceIdType.MESH,
            )

    pl.semaphore_wait(barrier, total)


def remote(src, dst, send_sem, recv_sem, axis, peer):
    return pltpu.make_async_remote_copy(
        src_ref=src, dst_ref=dst, send_sem=send_sem, recv_sem=recv_sem,
        device_id={axis: peer}, device_id_type=pl.DeviceIdType.MESH,
    )


def fused_kernel(chunks, subs, rows_ref, lists_ref, c_ref, b_ref, alpha_ref, own_ref, mirror_ref, *scratch):
    held, sent, xt = scratch[:chunks], scratch[chunks : 2 * chunks], scratch[2 * chunks : 2 * chunks + subs]
    (b_own, flat, a_own, a_all, xr, stack, own_out, mirror_out, list_own, list_all, table, picks,
     load_sem, c_own, c_send, c_recv, x_own, x_send, x_recv, l_own, l_send, l_recv, a_sem,
     up_send, up_recv, down_send, down_recv, y_send, y_recv, core_send, core_recv, t_sem,
     o_own, o_send, o_recv, m_own, m_send, m_recv) = scratch[2 * chunks + subs :]
    row_devices, row = lax.axis_size("row"), lax.axis_index("row")
    col_devices, col = lax.axis_size("col"), lax.axis_index("col")
    rows, columns = c_ref.shape
    tiles, depth, width = b_own.shape
    listed_b = depth // width
    slots, tile, _ = flat.shape
    groups = lists_ref.shape[1]
    listed = slots // groups
    chunk, strip = rows // chunks, columns // row_devices
    part = strip // subs
    chips = row_devices // 2
    per = tiles // chips
    stored = a_own.shape[0]
    lines = row_devices // 4
    chip, core = row // 2, lax.rem(row, 2)
    z, y = row // 4, lax.rem(chip, 2)
    units = [(c, 0, strip) for c in range(chunks - 1)]
    units += [(chunks - 1, s * part, part) for s in range(subs)]

    def own_c(c, t):
        return pltpu.make_async_copy(
            c_ref.at[pl.ds(c * chunk, chunk), pl.ds(pl.multiple_of(t * width, width), width)],
            held[c].at[col * tiles + t], c_own.at[c, t],
        )

    def send_c(c, off, t):
        return remote(
            c_ref.at[pl.ds(c * chunk, chunk), pl.ds(pl.multiple_of(t * width, width), width)],
            held[c].at[col * tiles + t], c_send.at[c, off - 1, t], c_recv.at[c, off - 1, t],
            "col", lax.rem(col + off, col_devices),
        )

    def send_x(u, off, peer):
        c, first, size = units[u]
        start = pl.multiple_of(peer * strip + first, 16)
        return remote(
            sent[c].at[pl.ds(start, size), :], xr.at[c, row, pl.ds(first, size), :],
            x_send.at[u, off - 1], x_recv.at[u, off - 1], "row", peer,
        )

    def own_x(u):
        c, first, size = units[u]
        start = pl.multiple_of(row * strip + first, 16)
        return pltpu.make_async_copy(
            sent[c].at[pl.ds(start, size), :], xr.at[c, row, pl.ds(first, size), :], x_own.at[u]
        )

    def send_own(s, off, peer):
        return remote(
            own_out.at[s, peer], own_ref.at[row, pl.ds(s * part, part), :],
            o_send.at[s, off - 1], o_recv.at[s, off - 1], "row", peer,
        )

    def stay_own(s):
        return pltpu.make_async_copy(
            own_out.at[s, row], own_ref.at[row, pl.ds(s * part, part), :], o_own.at[s]
        )

    def send_mirror(s, off):
        peer = lax.rem(col + off, col_devices)
        return remote(
            mirror_out.at[s, peer], mirror_ref.at[col, pl.ds(s * part, part), :],
            m_send.at[s, off - 1], m_recv.at[s, off - 1], "col", peer,
        )

    def stay_mirror(s):
        return pltpu.make_async_copy(
            mirror_out.at[s, col], mirror_ref.at[col, pl.ds(s * part, part), :], m_own.at[s]
        )

    def send_list(off):
        return remote(
            list_own, list_all.at[row], l_send.at[off - 1], l_recv.at[off - 1], "row",
            lax.rem(row + off, row_devices),
        )

    def reach(i):
        odd = lax.rem(i, 2)
        return chips // 2 + (1 - odd) * (i // 2) - odd * ((i + 1) // 2)

    def pair(i):
        return lax.rem(chip + reach(i), chips)

    def send_pair(send, i):
        for e in range(2):
            send(2 * reach(i) + e - core, 2 * pair(i) + e).start()

    partner, partner_off = row + 1 - 2 * core, 1 + core * (row_devices - 2)

    def block(at_z, at_y, at_core):
        return (at_z * 2 + at_y) * 2 + at_core

    def slab(at):
        return a_all.at[pl.ds(at * stored, stored)]

    def hand(source, at, send_sem, recv_sem, peer):
        return remote(source, slab(at), send_sem, recv_sem, "row", peer)

    def up(step, first=False):
        at = block(z - step, y, core)
        source = a_own if first else slab(at)
        return hand(source, at, up_send.at[step], up_recv.at[step], block(z + 1, y, core))

    def down(step, first=False):
        at = block(z + step, y, core)
        source = a_own if first else slab(at)
        return hand(source, at, down_send.at[step], down_recv.at[step], block(z - 1, y, core))

    def over_y(at_z, first=False):
        at = block(at_z, y, core)
        source = a_own if first else slab(at)
        return hand(source, at, y_send.at[at_z], y_recv.at[at_z], block(z, 1 - y, core))

    def over_core(at_z, at_y, first=False):
        at = block(at_z, at_y, core)
        source = a_own if first else slab(at)
        sem = at_z * 2 + at_y
        return hand(source, at, core_send.at[sem], core_recv.at[sem], block(z, y, 1 - core))

    def arrived(at, recv_sem, send_sem):
        hand(slab(at), at, send_sem, recv_sem, block(z, y, 1 - core)).wait_recv()

    def relay(step):
        @pl.when(z - 1 - step >= 0)
        def _():
            arrived(block(z - 1 - step, y, core), up_recv.at[step], up_send.at[step])
            if step + 1 < lines - 1:

                @pl.when(z + 1 < lines)
                def _():
                    up(step + 1).start()

            over_y(z - 1 - step).start()
            over_core(z - 1 - step, y).start()

        @pl.when(z + 1 + step < lines)
        def _():
            arrived(block(z + 1 + step, y, core), down_recv.at[step], down_send.at[step])
            if step + 1 < lines - 1:

                @pl.when(z >= 1)
                def _():
                    down(step + 1).start()

            over_y(z + 1 + step).start()
            over_core(z + 1 + step, y).start()

    def cross(step):
        at_z = lax.rem(z + step, lines)
        arrived(block(at_z, 1 - y, core), y_recv.at[at_z], y_send.at[at_z])
        over_core(at_z, 1 - y).start()

    def multiply(c, group):
        for q in range(per):
            j = group * per + q
            picked = [held[c][rows_ref[s, 0, j]] for s in range(listed_b)]
            product = lax.dot_general(
                b_own[j], jnp.concatenate(picked, axis=1), (((0,), (1,)), ((), ())),
                preferred_element_type=jnp.float32,
            )
            sent[c][pl.ds(pl.multiple_of(j * width, width), width), :] = product.astype(jnp.bfloat16)

    def make_table():
        total = list_all[0]
        for r in range(1, row_devices):
            total = total + list_all[r]
        square = (width, width)
        by_lane = jnp.broadcast_to(total[0:1], square)
        lane = lax.broadcasted_iota(jnp.int32, square, 1)
        sub = lax.broadcasted_iota(jnp.int32, square, 0)
        keys = by_lane * width + lane

        def count(mask):
            return jnp.sum(jnp.where(mask, 1, 0), axis=0, keepdims=True)

        rank = jnp.broadcast_to(count(keys.T < keys), square)
        hit = rank.T == lane
        by_sub = by_lane.T
        order = jnp.sum(jnp.where(hit, sub, 0), axis=0, keepdims=True)
        target = jnp.sum(jnp.where(hit, by_sub, 0), axis=0, keepdims=True)
        began = count(by_sub < target)
        source, slot = order // slots, order % slots
        table[0:1, :] = source * stored + slot
        table[1:2, :] = source * stored + slots + slot % listed
        table[2:3, :] = order // listed
        table[3:4, :] = jnp.where(lane[0:1] > began, 1, 0)
        table[4:5, :] = count(by_sub <= lane) - 1
        table[5:8, :] = jnp.zeros((3, width), jnp.int32)

    def prepare(s):
        lane = lax.broadcasted_iota(jnp.int32, (part, width), 1)
        low = lane < width // 2

        @pl.loop(0, row_devices)
        def _(r):
            cut = pl.ds(s * part, part)
            middle = xr[1, r, cut, :]
            blank = jnp.zeros_like(middle)
            xt[s][r * groups, :, 0:width] = xr[0, r, cut, :]
            xt[s][r * groups, :, width : 2 * width] = jnp.where(low, middle, blank)
            xt[s][r * groups + 1, :, 0:width] = xr[2, r, cut, :]
            xt[s][r * groups + 1, :, width : 2 * width] = jnp.where(low, blank, middle)

    def contract(s):
        def step(p, run):
            weights = jnp.concatenate([a_all[picks[0, p]], a_all[picks[1, p]]], axis=1)
            product = lax.dot_general(
                xt[s][picks[2, p]], weights, CONTRACT_LAST, preferred_element_type=jnp.float32
            )
            run = product + run * picks[3, p].astype(jnp.float32)
            stack[p] = run.astype(stack.dtype)
            return run

        lax.fori_loop(0, width, step, jnp.zeros((part, tile), jnp.float32), unroll=4)

    def assemble(s, k):
        found = [[stack[picks[4, g * row_devices + 2 * k + e]] for e in range(2)] for g in range(groups)]
        for e in range(2):
            own_out[s, 2 * k + e] = jnp.concatenate([found[g][e] for g in range(groups)], axis=1)
        for g in range(groups):
            start = pl.multiple_of(k * 2 * tile, width)
            mirror_out[s, g, :, pl.ds(start, 2 * tile)] = jnp.concatenate(found[g], axis=1)

    load_b = pltpu.make_async_copy(b_ref, b_own, load_sem.at[0])
    load_a = pltpu.make_async_copy(alpha_ref, flat, load_sem.at[1])
    load_a.start()
    for c in range(chunks):

        @pl.loop(0, tiles)
        def _(t):
            own_c(c, t).start()

        if c == 0:
            load_b.start()

    lane = lax.broadcasted_iota(jnp.int32, list_own.shape, 1)
    mine = jnp.zeros(list_own.shape, jnp.int32)
    for g in range(groups):
        for s in range(listed):
            mine = jnp.where(lane == row * slots + g * listed + s, lists_ref[0, g, 0, s], mine)
    list_own[...] = mine
    load_a.wait()
    for s in range(listed):
        first, second = flat[s], flat[listed + s]
        a_own[s] = first[:, :width]
        a_own[listed + s] = second[:, tile - width :]
        a_own[slots + s] = jnp.concatenate([first[:, width:], second[:, : tile - width]], axis=1)
    keep_list = pltpu.make_async_copy(list_own, list_all.at[row], l_own)
    keep_list.start()
    greet(("row", "col"))
    for c in range(chunks):
        for off in range(1, col_devices):

            @pl.loop(0, tiles)
            def _(t):
                send_c(c, off, t).start()

        if c == 0:

            @pl.loop(1, row_devices)
            def _(off):
                send_list(off).start()

            @pl.when(z + 1 < lines)
            def _():
                up(0, True).start()

            @pl.when(z >= 1)
            def _():
                down(0, True).start()

            over_y(z, True).start()
            over_core(z, y, True).start()

    keep_a = pltpu.make_async_copy(a_own, slab(row), a_sem)
    keep_a.start()
    load_b.wait()
    move_table = pltpu.make_async_copy(table, picks, t_sem)
    relayed = 0
    for c in range(chunks):
        if relayed < lines - 1:
            relay(relayed)
            relayed += 1

        @pl.loop(0, tiles)
        def _(t):
            own_c(c, t).wait()
            for off in range(1, col_devices):
                send_c(c, off, t).wait_recv()

        @pl.loop(0, chips)
        def _(i):
            multiply(c, pair(i))

            @pl.when(i > 0)
            def _():
                send_pair(functools.partial(send_x, c), i - 1)

        send_x(c, partner_off, partner).start()
        own_x(c).start()
        if c == chunks - 1:
            for s in range(1, subs):

                @pl.loop(0, chips - 1)
                def _(i):
                    send_pair(functools.partial(send_x, c + s), i)

                send_x(c + s, partner_off, partner).start()
                own_x(c + s).start()
        if c == 0:
            keep_list.wait()

            @pl.loop(1, row_devices)
            def _(off):
                send_list(off).wait_recv()

            make_table()
            move_table.start()
            cross(0)

    for step in range(relayed, lines - 1):
        relay(step)
    for step in range(1, lines):
        cross(step)
    keep_a.wait()
    move_table.wait()
    for at_z in range(lines):
        for at_y in range(2):
            sem = at_z * 2 + at_y
            arrived(block(at_z, at_y, 1 - core), core_recv.at[sem], core_send.at[sem])
    for s in range(subs):
        for u in range(chunks) if s == 0 else [chunks - 1 + s]:
            own_x(u).wait()

            @pl.loop(1, row_devices)
            def _(off):
                send_x(u, off, lax.rem(row + off, row_devices)).wait_recv()

        prepare(s)
        contract(s)

        @pl.loop(0, chips)
        def _(i):
            assemble(s, pair(i))

            @pl.when(i > 0)
            def _():
                send_pair(functools.partial(send_own, s), i - 1)

        send_own(s, partner_off, partner).start()
        for off in range(1, col_devices):
            send_mirror(s, off).start()
        stay_own(s).start()
        stay_mirror(s).start()

    for step in range(lines - 1):

        @pl.when((z - step >= 0) & (z + 1 < lines))
        def _():
            up(step, step == 0).wait_send()

        @pl.when((z + step < lines) & (z >= 1))
        def _():
            down(step, step == 0).wait_send()

    for at_z in range(lines):
        over_y(at_z).wait_send()
        for at_y in range(2):
            over_core(at_z, at_y).wait_send()

    for c in range(chunks):
        for off in range(1, col_devices):

            @pl.loop(0, tiles)
            def _(t):
                send_c(c, off, t).wait_send()

    @pl.loop(1, row_devices)
    def _(off):
        peer = lax.rem(row + off, row_devices)
        send_list(off).wait_send()
        for u in range(len(units)):
            send_x(u, off, peer).wait_send()
        for s in range(subs):
            send_own(s, off, peer).wait()

    for s in range(subs):
        stay_own(s).wait()
        stay_mirror(s).wait()
        for off in range(1, col_devices):
            send_mirror(s, off).wait()


def fused(c_matrix, beta_values, beta_rows, alpha_tiles, alpha_rows, row_devices, col_devices, subs):
    rows, columns = c_matrix.shape
    _, tiles, listed, width, _ = beta_values.shape
    slots, tile, _ = alpha_tiles.shape
    groups = alpha_rows.shape[1]
    chunks, strip = rows // width, columns // row_devices
    part, units, lines = strip // subs, rows // width - 1 + subs, row_devices // 4
    stored = slots * tile // width
    row_peers, col_peers = row_devices - 1, col_devices - 1
    dma, half = pltpu.SemaphoreType.DMA, jnp.bfloat16
    anywhere = pl.BlockSpec(memory_space=pl.ANY)
    scalars = pl.BlockSpec(memory_space=pltpu.SMEM)
    return pl.pallas_call(
        functools.partial(fused_kernel, chunks, subs),
        in_specs=[scalars, scalars, anywhere, anywhere, anywhere],
        out_specs=[anywhere, anywhere],
        out_shape=[
            jax.ShapeDtypeStruct((row_devices, strip, groups * tile), half),
            jax.ShapeDtypeStruct((col_devices, strip, row_devices * tile), half),
        ],
        scratch_shapes=[pltpu.VMEM((col_devices * tiles, width, width), half)] * chunks
        + [pltpu.VMEM((columns, width), half)] * chunks
        + [pltpu.VMEM((row_devices * groups, part, 2 * width), half)] * subs
        + [
            pltpu.VMEM((tiles, listed * width, width), half),
            pltpu.VMEM((slots, tile, tile), half),
            pltpu.VMEM((stored, tile, width), half),
            pltpu.VMEM((row_devices * stored, tile, width), half),
            pltpu.VMEM((chunks, row_devices, strip, width), half),
            pltpu.VMEM((row_devices * slots, part, tile), half),
            pltpu.VMEM((subs, row_devices, part, groups * tile), half),
            pltpu.VMEM((subs, groups, part, row_devices * tile), half),
            pltpu.VMEM((8, width), jnp.int32),
            pltpu.VMEM((row_devices, 8, width), jnp.int32),
            pltpu.VMEM((8, width), jnp.int32),
            pltpu.SMEM((8, width), jnp.int32),
            dma((2,)),
            dma((chunks, tiles)), dma((chunks, col_peers, tiles)), dma((chunks, col_peers, tiles)),
            dma((units,)), dma((units, row_peers)), dma((units, row_peers)),
            dma, dma((row_peers,)), dma((row_peers,)), dma,
        ]
        + [dma((lines - 1,))] * 4
        + [dma((lines,))] * 2
        + [dma((2 * lines,))] * 2
        + [
            dma,
            dma((subs,)), dma((subs, row_peers)), dma((subs, row_peers)),
            dma((subs,)), dma((subs, col_peers)), dma((subs, col_peers)),
        ],
        compiler_params=pltpu.CompilerParams(
            collective_id=0, has_side_effects=True, vmem_limit_bytes=60 << 20
        ),
        cost_estimate=pl.CostEstimate(flops=1 << 37, bytes_accessed=1 << 28, transcendentals=0),
        name="fused",
    )(
        jnp.transpose(beta_rows, (2, 0, 1)), alpha_rows, c_matrix,
        beta_values.reshape(tiles, listed * width, width), alpha_tiles,
    )


def per_device(c_matrix, beta_values, beta_rows, alpha_values, alpha_rows, gaps):
    row_devices, col_devices = lax.axis_size("row"), lax.axis_size("col")
    groups, stretch, columns = c_matrix.shape
    pairs, _, _, listed, tile, _ = alpha_values.shape
    rows, width = groups * stretch, beta_values.shape[-1]
    c_rows = c_matrix.reshape(rows, columns)
    alpha_tiles = alpha_values.reshape(pairs * groups, listed, tile, tile)
    strip, subs = columns // row_devices, 2
    own_kernels = pairs == 1 and groups == 2 and stretch == tile and 2 * tile == 3 * width
    own_kernels = own_kernels and row_devices % 4 == 0 and row_devices * groups * listed == width
    own_kernels = own_kernels and strip % (16 * subs) == 0 and 2 * strip % width == 0
    if own_kernels:
        own, mirror = fused(
            c_rows, beta_values, beta_rows, alpha_tiles.reshape(-1, tile, tile), alpha_rows,
            row_devices, col_devices, subs,
        )
    else:
        rows_all = lax.all_gather(alpha_rows.reshape(pairs * groups, listed), "row")
        alpha_all = lax.all_gather(alpha_tiles, "row")
        xt = beta_products(lax.all_gather(c_rows, "col"), beta_values, beta_rows)
        xt = jnp.moveaxis(xt.reshape(pairs, row_devices, stretch, rows), 1, 0)
        x_strip = lax.all_to_all(xt, "row", 0, 0)[None]
        own, mirror = alpha_products(alpha_all, rows_all, x_strip, groups)
        own = lax.all_to_all(own, "row", 0, 0)
        mirror = lax.all_to_all(mirror, "col", 0, 0)
    out = final(
        own.reshape(columns, groups * stretch),
        mirror.reshape(groups * stretch, columns),
        gaps.reshape(groups * stretch, columns),
    )
    return out.reshape(gaps.shape)


def solution(mesh):
    placed = (
        P(None, "row", "col"),
        P(None, "col", None, None, None),
        P(None, "col", None),
        P(None, None, "row", None, None, None),
        P(None, None, "row", None),
        P(None, "row", "col"),
    )
    return jax.shard_map(
        per_device, mesh=mesh, in_specs=placed, out_specs=P(None, "row", "col"), check_vma=False
    )
```

time: 185 us -> 162 us (0.88)
  the two profiles are of different devices: /device:TPU:0 before, /device:TPU:13 now
where the time goes in v1:
time: 162 us; the launch traced here: 160 us
  Pallas kernels  160 us (99%)
    pallas_call x1, Pallas kernels, fused(): pl.pallas_call(functools.partial(fused_kernel, chunks, subs), in_specs=[s...  152 us
    pallas_call x1, Pallas kernels, final(): pl.pallas_call(final_kernel, grid=(columns // block,), in_specs=[pl.Block...  8.27 us

profile of v1, /device:TPU:13, one launch (start us, length us, event | category | flops | bytes accessed | tf_op | source)
XLA Modules:
  0.0 160.0 jit_solution(7641952920258253577)
XLA Ops:
  0.0 151.7 %fused.1 = (bf16[16,192,384]{2,1,0:T(8,128)(2,1)}, bf16[2,192,3072]{2,1,0:T(8,128)(2,1)}) custom-call(s32[6,1,24]{2,1,0:T(1,128)} %bitcast.14, s32[1,2,1,4]{3,2,1,0:T(1,128)} %lists_ref.1, bf16[384,3072]{1,0:T(8,128)(2,1)} %bitcast.12, bf16[24,768,128]{2,1,0:T(8,128)(2,1)} %bitcast.11, bf16[8,192,192]{2,1,0:T(8,128)(2,1)} %bitcast.13), custom_call_target="tpu_custom_call" | custom-call | flops 137438953472 | bytes 268435456 | tf_op jit(solution)/shard_map/fused/pallas_call | solution.py:568
  151.7 8.3 %final.1 = f32[384,3072]{1,0:T(8,128)} custom-call(bf16[3072,384]{1,0:T(8,128)(2,1)} %bitcast.9, bf16[384,3072]{1,0:T(8,128)(2,1)} %bitcast.10, f32[384,3072]{1,0:T(8,128)} %bitcast.8), custom_call_target="tpu_custom_call" | custom-call | tf_op jit(solution)/shard_map/final/pallas_call | solution.py:123

commit v2 on v1

--- a/solution.py
+++ b/solution.py
@@ -8,6 +8,7 @@
 from jax.sharding import PartitionSpec as P
 
 CONTRACT_LAST = (((1,), (1,)), ((), ()))
+SHARE = 2
 
 
 def beta_kernel(listed, held, rows_ref, c_ref, b_ref, xt_ref):
@@ -130,12 +131,10 @@
     )(own, mirror, gaps)
 
 
-def greet(axes):
+def knock(axes):
     barrier = pltpu.get_barrier_semaphore()
-    total = 0
     for axis in axes:
         size, me = lax.axis_size(axis), lax.axis_index(axis)
-        total += size - 1
 
         @pl.loop(1, size)
         def _(off):
@@ -144,7 +143,10 @@
                 device_id_type=pl.DeviceIdType.MESH,
             )
 
-    pl.semaphore_wait(barrier, total)
+
+def enter(axes):
+    total = sum(lax.axis_size(axis) - 1 for axis in axes)
+    pl.semaphore_wait(pltpu.get_barrier_semaphore(), total)
 
 
 def remote(src, dst, send_sem, recv_sem, axis, peer):
@@ -154,11 +156,12 @@
     )
 
 
-def fused_kernel(chunks, subs, rows_ref, lists_ref, c_ref, b_ref, alpha_ref, own_ref, mirror_ref, *scratch):
+def fused_kernel(chunks, subs, share, rows_ref, lists_ref, c_ref, b_ref, alpha_ref, own_ref, mirror_ref, *scratch):
     held, sent, xt = scratch[:chunks], scratch[chunks : 2 * chunks], scratch[2 * chunks : 2 * chunks + subs]
     (b_own, flat, a_own, a_all, xr, stack, own_out, mirror_out, list_own, list_all, table, picks,
      load_sem, c_own, c_send, c_recv, x_own, x_send, x_recv, l_own, l_send, l_recv, a_sem,
-     up_send, up_recv, down_send, down_recv, y_send, y_recv, core_send, core_recv, t_sem,
+     up_send, up_recv, down_send, down_recv, y_send, y_recv, core_send, core_recv,
+     x_side, x_side_recv, core_side, core_side_recv, t_sem,
      o_own, o_send, o_recv, m_own, m_send, m_recv) = scratch[2 * chunks + subs :]
     row_devices, row = lax.axis_size("row"), lax.axis_index("row")
     col_devices, col = lax.axis_size("col"), lax.axis_index("col")
@@ -252,40 +255,55 @@
     def block(at_z, at_y, at_core):
         return (at_z * 2 + at_y) * 2 + at_core
 
-    def slab(at):
-        return a_all.at[pl.ds(at * stored, stored)]
-
-    def hand(source, at, send_sem, recv_sem, peer):
-        return remote(source, slab(at), send_sem, recv_sem, "row", peer)
-
-    def up(step, first=False):
+    def cut(ref, at, first, size):
+        return ref.at[pl.ds(at * stored + first, size)]
+
+    def hand(at, first, size, send_sem, recv_sem, peer, axis="row", source=None):
+        held_part = cut(a_all, at, first, size)
+        if source is not None:
+            held_part = source.at[pl.ds(first, size)]
+        return remote(held_part, cut(a_all, at, first, size), send_sem, recv_sem, axis, peer)
+
+    main = (col * share, stored - share)
+    gives, gets = (col * (stored - share), share), ((1 - col) * (stored - share), share)
+    other_core = block(z, y, 1 - core)
+
+    def up(step, source=None):
         at = block(z - step, y, core)
-        source = a_own if first else slab(at)
-        return hand(source, at, up_send.at[step], up_recv.at[step], block(z + 1, y, core))
-
-    def down(step, first=False):
+        return hand(at, *main, up_send.at[step], up_recv.at[step], block(z + 1, y, core), source=source)
+
+    def down(step, source=None):
         at = block(z + step, y, core)
-        source = a_own if first else slab(at)
-        return hand(source, at, down_send.at[step], down_recv.at[step], block(z - 1, y, core))
-
-    def over_y(at_z, first=False):
+        return hand(at, *main, down_send.at[step], down_recv.at[step], block(z - 1, y, core), source=source)
+
+    def over_y(at_z, source=None):
         at = block(at_z, y, core)
-        source = a_own if first else slab(at)
-        return hand(source, at, y_send.at[at_z], y_recv.at[at_z], block(z, 1 - y, core))
-
-    def over_core(at_z, at_y, first=False):
-        at = block(at_z, at_y, core)
-        source = a_own if first else slab(at)
-        sem = at_z * 2 + at_y
-        return hand(source, at, core_send.at[sem], core_recv.at[sem], block(z, y, 1 - core))
-
-    def arrived(at, recv_sem, send_sem):
-        hand(slab(at), at, send_sem, recv_sem, block(z, y, 1 - core)).wait_recv()
+        return hand(at, *main, y_send.at[at_z], y_recv.at[at_z], block(z, 1 - y, core), source=source)
+
+    def over_core(at_z, at_y, source=None):
+        at, sem = block(at_z, at_y, core), at_z * 2 + at_y
+        return hand(at, *main, core_send.at[sem], core_recv.at[sem], other_core, source=source)
+
+    def side_x(at_z, at_y):
+        at, sem = block(at_z, at_y, core), at_z * 2 + at_y
+        return hand(at, *gives, x_side.at[sem], x_side_recv.at[sem], 1 - col, "col")
+
+    def side_core(at_z, at_y, source=None):
+        at, sem = block(at_z, at_y, core), at_z * 2 + at_y
+        return hand(at, *gets, core_side.at[sem], core_side_recv.at[sem], other_core, source=source)
+
+    def arrived(at, span, recv_sem, send_sem):
+        hand(at, *span, send_sem, recv_sem, other_core).wait_recv()
+
+    def spread(at_z, at_y):
+        over_core(at_z, at_y).start()
+        if share:
+            side_x(at_z, at_y).start()
 
     def relay(step):
         @pl.when(z - 1 - step >= 0)
         def _():
-            arrived(block(z - 1 - step, y, core), up_recv.at[step], up_send.at[step])
+            arrived(block(z - 1 - step, y, core), main, up_recv.at[step], up_send.at[step])
             if step + 1 < lines - 1:
 
                 @pl.when(z + 1 < lines)
@@ -293,11 +311,11 @@
                     up(step + 1).start()
 
             over_y(z - 1 - step).start()
-            over_core(z - 1 - step, y).start()
+            spread(z - 1 - step, y)
 
         @pl.when(z + 1 + step < lines)
         def _():
-            arrived(block(z + 1 + step, y, core), down_recv.at[step], down_send.at[step])
+            arrived(block(z + 1 + step, y, core), main, down_recv.at[step], down_send.at[step])
             if step + 1 < lines - 1:
 
                 @pl.when(z >= 1)
@@ -305,12 +323,23 @@
                     down(step + 1).start()
 
             over_y(z + 1 + step).start()
-            over_core(z + 1 + step, y).start()
+            spread(z + 1 + step, y)
 
     def cross(step):
         at_z = lax.rem(z + step, lines)
-        arrived(block(at_z, 1 - y, core), y_recv.at[at_z], y_send.at[at_z])
-        over_core(at_z, 1 - y).start()
+        arrived(block(at_z, 1 - y, core), main, y_recv.at[at_z], y_send.at[at_z])
+        spread(at_z, 1 - y)
+
+    def others(body):
+        for step in range(1, lines):
+            body(lax.rem(z + step, lines), y)
+        for step in range(lines):
+            body(lax.rem(z + step, lines), 1 - y)
+
+    def side_arrived(at_z, at_y):
+        sem = at_z * 2 + at_y
+        hand(block(at_z, at_y, core), *gets, x_side.at[sem], x_side_recv.at[sem], 1 - col, "col").wait_recv()
+        side_core(at_z, at_y).start()
 
     def multiply(c, group):
         for q in range(per):
@@ -386,15 +415,7 @@
     load_b = pltpu.make_async_copy(b_ref, b_own, load_sem.at[0])
     load_a = pltpu.make_async_copy(alpha_ref, flat, load_sem.at[1])
     load_a.start()
-    for c in range(chunks):
-
-        @pl.loop(0, tiles)
-        def _(t):
-            own_c(c, t).start()
-
-        if c == 0:
-            load_b.start()
-
+    knock(("row", "col"))
     lane = lax.broadcasted_iota(jnp.int32, list_own.shape, 1)
     mine = jnp.zeros(list_own.shape, jnp.int32)
     for g in range(groups):
@@ -408,8 +429,21 @@
         a_own[listed + s] = second[:, tile - width :]
         a_own[slots + s] = jnp.concatenate([first[:, width:], second[:, : tile - width]], axis=1)
     keep_list = pltpu.make_async_copy(list_own, list_all.at[row], l_own)
-    keep_list.start()
-    greet(("row", "col"))
+    keep_a = pltpu.make_async_copy(a_own, cut(a_all, row, 0, stored), a_sem)
+    enter(("row", "col"))
+
+    @pl.when(z + 1 < lines)
+    def _():
+        up(0, a_own).start()
+
+    @pl.when(z >= 1)
+    def _():
+        down(0, a_own).start()
+
+    over_y(z, a_own).start()
+    over_core(z, y, a_own).start()
+    if share:
+        side_core(z, y, a_own).start()
     for c in range(chunks):
         for off in range(1, col_devices):
 
@@ -423,19 +457,14 @@
             def _(off):
                 send_list(off).start()
 
-            @pl.when(z + 1 < lines)
-            def _():
-                up(0, True).start()
-
-            @pl.when(z >= 1)
-            def _():
-                down(0, True).start()
-
-            over_y(z, True).start()
-            over_core(z, y, True).start()
-
-    keep_a = pltpu.make_async_copy(a_own, slab(row), a_sem)
-    keep_a.start()
+            keep_list.start()
+            keep_a.start()
+            load_b.start()
+
+        @pl.loop(0, tiles)
+        def _(t):
+            own_c(c, t).start()
+
     load_b.wait()
     move_table = pltpu.make_async_copy(table, picks, t_sem)
     relayed = 0
@@ -484,12 +513,16 @@
         relay(step)
     for step in range(1, lines):
         cross(step)
+    if share:
+        others(side_arrived)
     keep_a.wait()
     move_table.wait()
     for at_z in range(lines):
         for at_y in range(2):
-            sem = at_z * 2 + at_y
-            arrived(block(at_z, at_y, 1 - core), core_recv.at[sem], core_send.at[sem])
+            at, sem = block(at_z, at_y, 1 - core), at_z * 2 + at_y
+            arrived(at, main, core_recv.at[sem], core_send.at[sem])
+            if share:
+                arrived(at, gets, core_side_recv.at[sem], core_side.at[sem])
     for s in range(subs):
         for u in range(chunks) if s == 0 else [chunks - 1 + s]:
             own_x(u).wait()
@@ -519,17 +552,21 @@
 
         @pl.when((z - step >= 0) & (z + 1 < lines))
         def _():
-            up(step, step == 0).wait_send()
+            up(step).wait_send()
 
         @pl.when((z + step < lines) & (z >= 1))
         def _():
-            down(step, step == 0).wait_send()
+            down(step).wait_send()
 
     for at_z in range(lines):
         over_y(at_z).wait_send()
         for at_y in range(2):
             over_core(at_z, at_y).wait_send()
-
+            if share:
+                side_core(at_z, at_y).wait_send()
+
+    if share:
+        others(lambda at_z, at_y: side_x(at_z, at_y).wait_send())
     for c in range(chunks):
         for off in range(1, col_devices):
 
@@ -553,7 +590,7 @@
             send_mirror(s, off).wait()
 
 
-def fused(c_matrix, beta_values, beta_rows, alpha_tiles, alpha_rows, row_devices, col_devices, subs):
+def fused(c_matrix, beta_values, beta_rows, alpha_tiles, alpha_rows, row_devices, col_devices, subs, share):
     rows, columns = c_matrix.shape
     _, tiles, listed, width, _ = beta_values.shape
     slots, tile, _ = alpha_tiles.shape
@@ -566,7 +603,7 @@
     anywhere = pl.BlockSpec(memory_space=pl.ANY)
     scalars = pl.BlockSpec(memory_space=pltpu.SMEM)
     return pl.pallas_call(
-        functools.partial(fused_kernel, chunks, subs),
+        functools.partial(fused_kernel, chunks, subs, share),
         in_specs=[scalars, scalars, anywhere, anywhere, anywhere],
         out_specs=[anywhere, anywhere],
         out_shape=[
@@ -596,7 +633,7 @@
         ]
         + [dma((lines - 1,))] * 4
         + [dma((lines,))] * 2
-        + [dma((2 * lines,))] * 2
+        + [dma((2 * lines,))] * 6
         + [
             dma,
             dma((subs,)), dma((subs, row_peers)), dma((subs, row_peers)),
@@ -627,7 +664,7 @@
     if own_kernels:
         own, mirror = fused(
             c_rows, beta_values, beta_rows, alpha_tiles.reshape(-1, tile, tile), alpha_rows,
-            row_devices, col_devices, subs,
+            row_devices, col_devices, subs, SHARE,
         )
     else:
         rows_all = lax.all_gather(alpha_rows.reshape(pairs * groups, listed), "row")

time: 162 us -> 153 us (0.944)
  Pallas kernels: 160 us -> 152 us
    pallas_call x1, Pallas kernels: 152 us -> 143 us  [fused(): pl.pallas_call(functools.partial(fused_kernel, chunks, subs, share), in_s...]
where the time goes in v2:
time: 153 us; the launch traced here: 152 us
  Pallas kernels  152 us (99%)
    pallas_call x1, Pallas kernels, fused(): pl.pallas_call(functools.partial(fused_kernel, chunks, subs, share), in_s...  143 us
    pallas_call x1, Pallas kernels, final(): pl.pallas_call(final_kernel, grid=(columns // block,), in_specs=[pl.Block...  8.27 us

profile of v2, /device:TPU:13, one launch (start us, length us, event | category | flops | bytes accessed | tf_op | source)
XLA Modules:
  0.0 151.7 jit_solution(16822920175696735126)
XLA Ops:
  0.0 143.4 %fused.1 = (bf16[16,192,384]{2,1,0:T(8,128)(2,1)}, bf16[2,192,3072]{2,1,0:T(8,128)(2,1)}) custom-call(s32[6,1,24]{2,1,0:T(1,128)} %bitcast.14, s32[1,2,1,4]{3,2,1,0:T(1,128)} %lists_ref.1, bf16[384,3072]{1,0:T(8,128)(2,1)} %bitcast.12, bf16[24,768,128]{2,1,0:T(8,128)(2,1)} %bitcast.11, bf16[8,192,192]{2,1,0:T(8,128)(2,1)} %bitcast.13), custom_call_target="tpu_custom_call" | custom-call | flops 137438953472 | bytes 268435456 | tf_op jit(solution)/shard_map/fused/pallas_call | solution.py:605
  143.4 8.3 %final.1 = f32[384,3072]{1,0:T(8,128)} custom-call(bf16[3072,384]{1,0:T(8,128)(2,1)} %bitcast.9, bf16[384,3072]{1,0:T(8,128)(2,1)} %bitcast.10, f32[384,3072]{1,0:T(8,128)} %bitcast.8), custom_call_target="tpu_custom_call" | custom-call | tf_op jit(solution)/shard_map/final/pallas_call | solution.py:124

commit v3 on v2

--- a/solution.py
+++ b/solution.py
@@ -112,21 +112,49 @@
     )(rows_all, alpha_all, x_strip)
 
 
-def final_kernel(own_ref, mirror_ref, gaps_ref, out_ref):
-    own = own_ref[...].T.astype(jnp.float32)
-    out_ref[...] = (own + mirror_ref[...].astype(jnp.float32)) / gaps_ref[...]
+def final_kernel(block, own_ref, mirror_ref, gaps_ref, out_ref, own, mirror, gaps, out, in_sem, out_sem):
+    steps = out.shape[1] // block
+
+    def fetch(i):
+        span = pl.ds(i * block, block)
+        pairs = (
+            (gaps_ref.at[:, span], gaps.at[:, span]), (own_ref.at[span, :], own.at[span, :]),
+            (mirror_ref.at[:, span], mirror.at[:, span]),
+        )
+        return [pltpu.make_async_copy(*pair, in_sem.at[n, i]) for n, pair in enumerate(pairs)]
+
+    def store(i):
+        span = pl.ds(i * block, block)
+        return pltpu.make_async_copy(out.at[:, span], out_ref.at[:, span], out_sem.at[i])
+
+    for i in range(steps):
+        for copy in fetch(i):
+            copy.start()
+    for i in range(steps):
+        for copy in fetch(i):
+            copy.wait()
+        span = slice(i * block, (i + 1) * block)
+        turned = own[span, :].T.astype(jnp.float32)
+        out[:, span] = (turned + mirror[:, span].astype(jnp.float32)) / gaps[:, span]
+        store(i).start()
+    for i in range(steps):
+        store(i).wait()
 
 
 def final(own, mirror, gaps):
     rows, columns = gaps.shape
-    block = next(n for n in (384, 256, 128) if columns % n == 0)
-    wide = pl.BlockSpec((rows, block), lambda i: (0, i))
+    block = next(n for n in (768, 384, 256, 128) if columns % n == 0)
+    dma, anywhere = pltpu.SemaphoreType.DMA, pl.BlockSpec(memory_space=pl.ANY)
     return pl.pallas_call(
-        final_kernel,
-        grid=(columns // block,),
-        in_specs=[pl.BlockSpec((block, rows), lambda i: (i, 0)), wide, wide],
-        out_specs=wide,
+        functools.partial(final_kernel, block),
+        in_specs=[anywhere] * 3,
+        out_specs=anywhere,
         out_shape=jax.ShapeDtypeStruct((rows, columns), jnp.float32),
+        scratch_shapes=[
+            pltpu.VMEM(own.shape, own.dtype), pltpu.VMEM(mirror.shape, mirror.dtype),
+            pltpu.VMEM(gaps.shape, gaps.dtype), pltpu.VMEM(gaps.shape, gaps.dtype),
+            dma((3, columns // block)), dma((columns // block,)),
+        ],
         name="final",
     )(own, mirror, gaps)
 
@@ -402,7 +430,7 @@
             stack[p] = run.astype(stack.dtype)
             return run
 
-        lax.fori_loop(0, width, step, jnp.zeros((part, tile), jnp.float32), unroll=4)
+        lax.fori_loop(0, width, step, jnp.zeros((part, tile), jnp.float32), unroll=16)
 
     def assemble(s, k):
         found = [[stack[picks[4, g * row_devices + 2 * k + e]] for e in range(2)] for g in range(groups)]

time: 153 us -> 147 us (0.961)
  Pallas kernels: 152 us -> 146 us
    pallas_call x1, Pallas kernels: 143 us -> 140 us  [fused(): pl.pallas_call(functools.partial(fused_kernel, chunks, subs, share), in_s...]
    pallas_call x1, Pallas kernels: 8.27 us -> 5.97 us  [final(): pl.pallas_call(functools.partial(final_kernel, block), in_specs=[anywhere...]
where the time goes in v3:
time: 147 us; the launch traced here: 146 us
  Pallas kernels  146 us (99%)
    pallas_call x1, Pallas kernels, fused(): pl.pallas_call(functools.partial(fused_kernel, chunks, subs, share), in_s...  140 us
    pallas_call x1, Pallas kernels, final(): pl.pallas_call(functools.partial(final_kernel, block), in_specs=[anywhere...  5.97 us

profile of v3, /device:TPU:13, one launch (start us, length us, event | category | flops | bytes accessed | tf_op | source)
XLA Modules:
  0.0 145.9 jit_solution(4691460244252340660)
XLA Ops:
  0.0 140.0 %fused.1 = (bf16[16,192,384]{2,1,0:T(8,128)(2,1)}, bf16[2,192,3072]{2,1,0:T(8,128)(2,1)}) custom-call(s32[6,1,24]{2,1,0:T(1,128)} %bitcast.14, s32[1,2,1,4]{3,2,1,0:T(1,128)} %lists_ref.1, bf16[384,3072]{1,0:T(8,128)(2,1)} %bitcast.12, bf16[24,768,128]{2,1,0:T(8,128)(2,1)} %bitcast.11, bf16[8,192,192]{2,1,0:T(8,128)(2,1)} %bitcast.13), custom_call_target="tpu_custom_call" | custom-call | flops 137438953472 | bytes 268435456 | tf_op jit(solution)/shard_map/fused/pallas_call | solution.py:633
  140.0 6.0 %final.1 = f32[384,3072]{1,0:T(8,128)} custom-call(bf16[3072,384]{1,0:T(8,128)(2,1)} %bitcast.9, bf16[384,3072]{1,0:T(8,128)(2,1)} %bitcast.10, f32[384,3072]{1,0:T(8,128)} %bitcast.8), custom_call_target="tpu_custom_call" | custom-call | tf_op jit(solution)/shard_map/final/pallas_call | solution.py:148

commit v4 on v3

--- a/solution.py
+++ b/solution.py
@@ -159,24 +159,6 @@
     )(own, mirror, gaps)
 
 
-def knock(axes):
-    barrier = pltpu.get_barrier_semaphore()
-    for axis in axes:
-        size, me = lax.axis_size(axis), lax.axis_index(axis)
-
-        @pl.loop(1, size)
-        def _(off):
-            pl.semaphore_signal(
-                barrier, inc=1, device_id={axis: lax.rem(me + off, size)},
-                device_id_type=pl.DeviceIdType.MESH,
-            )
-
-
-def enter(axes):
-    total = sum(lax.axis_size(axis) - 1 for axis in axes)
-    pl.semaphore_wait(pltpu.get_barrier_semaphore(), total)
-
-
 def remote(src, dst, send_sem, recv_sem, axis, peer):
     return pltpu.make_async_remote_copy(
         src_ref=src, dst_ref=dst, send_sem=send_sem, recv_sem=recv_sem,
@@ -190,7 +172,7 @@
      load_sem, c_own, c_send, c_recv, x_own, x_send, x_recv, l_own, l_send, l_recv, a_sem,
      up_send, up_recv, down_send, down_recv, y_send, y_recv, core_send, core_recv,
      x_side, x_side_recv, core_side, core_side_recv, t_sem,
-     o_own, o_send, o_recv, m_own, m_send, m_recv) = scratch[2 * chunks + subs :]
+     o_own, o_send, o_recv, m_own, m_send, m_recv, rounds) = scratch[2 * chunks + subs :]
     row_devices, row = lax.axis_size("row"), lax.axis_index("row")
     col_devices, col = lax.axis_size("col"), lax.axis_index("col")
     rows, columns = c_ref.shape
@@ -278,10 +260,37 @@
         for e in range(2):
             send(2 * reach(i) + e - core, 2 * pair(i) + e).start()
 
-    partner, partner_off = row + 1 - 2 * core, 1 + core * (row_devices - 2)
-
     def block(at_z, at_y, at_core):
         return (at_z * 2 + at_y) * 2 + at_core
+
+    def neighbours(act):
+        act("col", 1 - col)
+        act("row", block(z, y, 1 - core))
+        act("row", block(z, 1 - y, core))
+
+        @pl.when(z >= 1)
+        def _():
+            act("row", block(z - 1, y, core))
+
+        @pl.when(z + 1 < lines)
+        def _():
+            act("row", block(z + 1, y, core))
+
+    inner = lax.min(z, 1) + lax.min(lines - 1 - z, 1)
+
+    def signal_near(sem):
+        def act(axis, peer):
+            pl.semaphore_signal(
+                sem, inc=1, device_id={axis: peer}, device_id_type=pl.DeviceIdType.MESH
+            )
+
+        neighbours(act)
+
+    def meet(sem):
+        signal_near(sem)
+        pl.semaphore_wait(sem, 3 + inner)
+
+    partner, partner_off = row + 1 - 2 * core, 1 + core * (row_devices - 2)
 
     def cut(ref, at, first, size):
         return ref.at[pl.ds(at * stored + first, size)]
@@ -443,7 +452,8 @@
     load_b = pltpu.make_async_copy(b_ref, b_own, load_sem.at[0])
     load_a = pltpu.make_async_copy(alpha_ref, flat, load_sem.at[1])
     load_a.start()
-    knock(("row", "col"))
+    barrier = pltpu.get_barrier_semaphore()
+    signal_near(barrier)
     lane = lax.broadcasted_iota(jnp.int32, list_own.shape, 1)
     mine = jnp.zeros(list_own.shape, jnp.int32)
     for g in range(groups):
@@ -458,7 +468,7 @@
         a_own[slots + s] = jnp.concatenate([first[:, width:], second[:, : tile - width]], axis=1)
     keep_list = pltpu.make_async_copy(list_own, list_all.at[row], l_own)
     keep_a = pltpu.make_async_copy(a_own, cut(a_all, row, 0, stored), a_sem)
-    enter(("row", "col"))
+    pl.semaphore_wait(barrier, 3 + inner)
 
     @pl.when(z + 1 < lines)
     def _():
@@ -480,11 +490,6 @@
                 send_c(c, off, t).start()
 
         if c == 0:
-
-            @pl.loop(1, row_devices)
-            def _(off):
-                send_list(off).start()
-
             keep_list.start()
             keep_a.start()
             load_b.start()
@@ -492,6 +497,13 @@
         @pl.loop(0, tiles)
         def _(t):
             own_c(c, t).start()
+
+    for n in range(lines):
+        meet(rounds.at[n])
+
+    @pl.loop(1, row_devices)
+    def _(off):
+        send_list(off).start()
 
     load_b.wait()
     move_table = pltpu.make_async_copy(table, picks, t_sem)
@@ -666,6 +678,7 @@
             dma,
             dma((subs,)), dma((subs, row_peers)), dma((subs, row_peers)),
             dma((subs,)), dma((subs, col_peers)), dma((subs, col_peers)),
+            pltpu.SemaphoreType.REGULAR((lines,)),
         ],
         compiler_params=pltpu.CompilerParams(
             collective_id=0, has_side_effects=True, vmem_limit_bytes=60 << 20

time: 147 us -> 145 us (0.986)
  Pallas kernels: 146 us -> 144 us
    pallas_call x1, Pallas kernels: 140 us -> 138 us  [fused(): pl.pallas_call(functools.partial(fused_kernel, chunks, subs, share), in_s...]
where the time goes in v4:
time: 145 us; the launch traced here: 144 us
  Pallas kernels  144 us (99%)
    pallas_call x1, Pallas kernels, fused(): pl.pallas_call(functools.partial(fused_kernel, chunks, subs, share), in_s...  138 us
    pallas_call x1, Pallas kernels, final(): pl.pallas_call(functools.partial(final_kernel, block), in_specs=[anywhere...  5.97 us

profile of v4, /device:TPU:13, one launch (start us, length us, event | category | flops | bytes accessed | tf_op | source)
XLA Modules:
  0.0 144.0 jit_solution(17258575826364139416)
XLA Ops:
  0.0 138.0 %fused.1 = (bf16[16,192,384]{2,1,0:T(8,128)(2,1)}, bf16[2,192,3072]{2,1,0:T(8,128)(2,1)}) custom-call(s32[6,1,24]{2,1,0:T(1,128)} %bitcast.14, s32[1,2,1,4]{3,2,1,0:T(1,128)} %lists_ref.1, bf16[384,3072]{1,0:T(8,128)(2,1)} %bitcast.12, bf16[24,768,128]{2,1,0:T(8,128)(2,1)} %bitcast.11, bf16[8,192,192]{2,1,0:T(8,128)(2,1)} %bitcast.13), custom_call_target="tpu_custom_call" | custom-call | flops 137438953472 | bytes 268435456 | tf_op jit(solution)/shard_map/fused/pallas_call | solution.py:645
  138.0 6.0 %final.1 = f32[384,3072]{1,0:T(8,128)} custom-call(bf16[3072,384]{1,0:T(8,128)(2,1)} %bitcast.9, bf16[384,3072]{1,0:T(8,128)(2,1)} %bitcast.10, f32[384,3072]{1,0:T(8,128)} %bitcast.8), custom_call_target="tpu_custom_call" | custom-call | tf_op jit(solution)/shard_map/final/pallas_call | solution.py:148

commit v5 on v4

--- a/solution.py
+++ b/solution.py
@@ -8,7 +8,7 @@
 from jax.sharding import PartitionSpec as P
 
 CONTRACT_LAST = (((1,), (1,)), ((), ()))
-SHARE = 2
+SHARE = (2, 2)
 
 
 def beta_kernel(listed, held, rows_ref, c_ref, b_ref, xt_ref):
@@ -112,27 +112,14 @@
     )(rows_all, alpha_all, x_strip)
 
 
-def final_kernel(block, own_ref, mirror_ref, gaps_ref, out_ref, own, mirror, gaps, out, in_sem, out_sem):
+def final_kernel(block, own, mirror, gaps, out_ref, out, out_sem):
     steps = out.shape[1] // block
-
-    def fetch(i):
-        span = pl.ds(i * block, block)
-        pairs = (
-            (gaps_ref.at[:, span], gaps.at[:, span]), (own_ref.at[span, :], own.at[span, :]),
-            (mirror_ref.at[:, span], mirror.at[:, span]),
-        )
-        return [pltpu.make_async_copy(*pair, in_sem.at[n, i]) for n, pair in enumerate(pairs)]
 
     def store(i):
         span = pl.ds(i * block, block)
         return pltpu.make_async_copy(out.at[:, span], out_ref.at[:, span], out_sem.at[i])
 
     for i in range(steps):
-        for copy in fetch(i):
-            copy.start()
-    for i in range(steps):
-        for copy in fetch(i):
-            copy.wait()
         span = slice(i * block, (i + 1) * block)
         turned = own[span, :].T.astype(jnp.float32)
         out[:, span] = (turned + mirror[:, span].astype(jnp.float32)) / gaps[:, span]
@@ -143,18 +130,17 @@
 
 def final(own, mirror, gaps):
     rows, columns = gaps.shape
-    block = next(n for n in (768, 384, 256, 128) if columns % n == 0)
-    dma, anywhere = pltpu.SemaphoreType.DMA, pl.BlockSpec(memory_space=pl.ANY)
+    block = next(n for n in (384, 256, 128) if columns % n == 0)
+    whole = pl.BlockSpec(memory_space=pltpu.VMEM)
     return pl.pallas_call(
         functools.partial(final_kernel, block),
-        in_specs=[anywhere] * 3,
-        out_specs=anywhere,
+        in_specs=[whole] * 3,
+        out_specs=pl.BlockSpec(memory_space=pl.ANY),
         out_shape=jax.ShapeDtypeStruct((rows, columns), jnp.float32),
         scratch_shapes=[
-            pltpu.VMEM(own.shape, own.dtype), pltpu.VMEM(mirror.shape, mirror.dtype),
-            pltpu.VMEM(gaps.shape, gaps.dtype), pltpu.VMEM(gaps.shape, gaps.dtype),
-            dma((3, columns // block)), dma((columns // block,)),
+            pltpu.VMEM(gaps.shape, gaps.dtype), pltpu.SemaphoreType.DMA((columns // block,)),
         ],
+        compiler_params=pltpu.CompilerParams(vmem_limit_bytes=20 << 20),
         name="final",
     )(own, mirror, gaps)
 
@@ -189,8 +175,8 @@
     lines = row_devices // 4
     chip, core = row // 2, lax.rem(row, 2)
     z, y = row // 4, lax.rem(chip, 2)
-    units = [(c, 0, strip) for c in range(chunks - 1)]
-    units += [(chunks - 1, s * part, part) for s in range(subs)]
+    units = [(c, s * part, part) for s in range(subs) for c in range(chunks)]
+    straight, turned = range(2, chips, 2), range(1, chips, 2)
 
     def own_c(c, t):
         return pltpu.make_async_copy(
@@ -290,6 +276,14 @@
         signal_near(sem)
         pl.semaphore_wait(sem, 3 + inner)
 
+    def send_later(u, steps):
+        for o in steps:
+            for e in range(2):
+                send_x(u, 2 * o + e - core, 2 * lax.rem(chip + o, chips) + e).start()
+        if steps == straight:
+            send_x(u, partner_off, partner).start()
+            own_x(u).start()
+
     partner, partner_off = row + 1 - 2 * core, 1 + core * (row_devices - 2)
 
     def cut(ref, at, first, size):
@@ -301,46 +295,60 @@
             held_part = source.at[pl.ds(first, size)]
         return remote(held_part, cut(a_all, at, first, size), send_sem, recv_sem, axis, peer)
 
-    main = (col * share, stored - share)
-    gives, gets = (col * (stored - share), share), ((1 - col) * (stored - share), share)
+    def main(same):
+        part_share = share[0] if same else share[1]
+        return col * part_share, stored - part_share
+
+    def gives(same):
+        part_share = share[0] if same else share[1]
+        return col * (stored - part_share), part_share
+
+    def gets(same):
+        part_share = share[0] if same else share[1]
+        return (1 - col) * (stored - part_share), part_share
+
+    def place(at_z, same):
+        at_y = y if same else 1 - y
+        return block(at_z, at_y, core), at_z * 2 + at_y
+
     other_core = block(z, y, 1 - core)
 
     def up(step, source=None):
         at = block(z - step, y, core)
-        return hand(at, *main, up_send.at[step], up_recv.at[step], block(z + 1, y, core), source=source)
+        return hand(at, *main(True), up_send.at[step], up_recv.at[step], block(z + 1, y, core), source=source)
 
     def down(step, source=None):
         at = block(z + step, y, core)
-        return hand(at, *main, down_send.at[step], down_recv.at[step], block(z - 1, y, core), source=source)
+        return hand(at, *main(True), down_send.at[step], down_recv.at[step], block(z - 1, y, core), source=source)
 
     def over_y(at_z, source=None):
         at = block(at_z, y, core)
-        return hand(at, *main, y_send.at[at_z], y_recv.at[at_z], block(z, 1 - y, core), source=source)
-
-    def over_core(at_z, at_y, source=None):
-        at, sem = block(at_z, at_y, core), at_z * 2 + at_y
-        return hand(at, *main, core_send.at[sem], core_recv.at[sem], other_core, source=source)
-
-    def side_x(at_z, at_y):
-        at, sem = block(at_z, at_y, core), at_z * 2 + at_y
-        return hand(at, *gives, x_side.at[sem], x_side_recv.at[sem], 1 - col, "col")
-
-    def side_core(at_z, at_y, source=None):
-        at, sem = block(at_z, at_y, core), at_z * 2 + at_y
-        return hand(at, *gets, core_side.at[sem], core_side_recv.at[sem], other_core, source=source)
+        return hand(at, *main(False), y_send.at[at_z], y_recv.at[at_z], block(z, 1 - y, core), source=source)
+
+    def over_core(at_z, same, source=None):
+        at, sem = place(at_z, same)
+        return hand(at, *main(same), core_send.at[sem], core_recv.at[sem], other_core, source=source)
+
+    def side_x(at_z, same):
+        at, sem = place(at_z, same)
+        return hand(at, *gives(same), x_side.at[sem], x_side_recv.at[sem], 1 - col, "col")
+
+    def side_core(at_z, same, source=None):
+        at, sem = place(at_z, same)
+        return hand(at, *gets(same), core_side.at[sem], core_side_recv.at[sem], other_core, source=source)
 
     def arrived(at, span, recv_sem, send_sem):
         hand(at, *span, send_sem, recv_sem, other_core).wait_recv()
 
-    def spread(at_z, at_y):
-        over_core(at_z, at_y).start()
-        if share:
-            side_x(at_z, at_y).start()
+    def spread(at_z, same):
+        over_core(at_z, same).start()
+        if gives(same)[1]:
+            side_x(at_z, same).start()
 
     def relay(step):
         @pl.when(z - 1 - step >= 0)
         def _():
-            arrived(block(z - 1 - step, y, core), main, up_recv.at[step], up_send.at[step])
+            arrived(block(z - 1 - step, y, core), main(True), up_recv.at[step], up_send.at[step])
             if step + 1 < lines - 1:
 
                 @pl.when(z + 1 < lines)
@@ -348,11 +356,11 @@
                     up(step + 1).start()
 
             over_y(z - 1 - step).start()
-            spread(z - 1 - step, y)
+            spread(z - 1 - step, True)
 
         @pl.when(z + 1 + step < lines)
         def _():
-            arrived(block(z + 1 + step, y, core), main, down_recv.at[step], down_send.at[step])
+            arrived(block(z + 1 + step, y, core), main(True), down_recv.at[step], down_send.at[step])
             if step + 1 < lines - 1:
 
                 @pl.when(z >= 1)
@@ -360,23 +368,22 @@
                     down(step + 1).start()
 
             over_y(z + 1 + step).start()
-            spread(z + 1 + step, y)
+            spread(z + 1 + step, True)
 
     def cross(step):
         at_z = lax.rem(z + step, lines)
-        arrived(block(at_z, 1 - y, core), main, y_recv.at[at_z], y_send.at[at_z])
-        spread(at_z, 1 - y)
+        arrived(block(at_z, 1 - y, core), main(False), y_recv.at[at_z], y_send.at[at_z])
+        spread(at_z, False)
 
     def others(body):
-        for step in range(1, lines):
-            body(lax.rem(z + step, lines), y)
-        for step in range(lines):
-            body(lax.rem(z + step, lines), 1 - y)
-
-    def side_arrived(at_z, at_y):
-        sem = at_z * 2 + at_y
-        hand(block(at_z, at_y, core), *gets, x_side.at[sem], x_side_recv.at[sem], 1 - col, "col").wait_recv()
-        side_core(at_z, at_y).start()
+        for same, first in ((True, 1), (False, 0)):
+            if gives(same)[1]:
+                for step in range(first, lines):
+                    body(lax.rem(z + step, lines), same)
+
+    def side_arrived(at_z, same):
+        side_x(at_z, same).wait_recv()
+        side_core(at_z, same).start()
 
     def multiply(c, group):
         for q in range(per):
@@ -479,9 +486,9 @@
         down(0, a_own).start()
 
     over_y(z, a_own).start()
-    over_core(z, y, a_own).start()
-    if share:
-        side_core(z, y, a_own).start()
+    over_core(z, True, a_own).start()
+    if share[0]:
+        side_core(z, True, a_own).start()
     for c in range(chunks):
         for off in range(1, col_devices):
 
@@ -507,6 +514,7 @@
 
     load_b.wait()
     move_table = pltpu.make_async_copy(table, picks, t_sem)
+    now, later = [[0], [1], [2]], [[(3, straight)], [(3, turned), (4, straight)], [(5, straight), (4, turned), (5, turned)]]
     relayed = 0
     for c in range(chunks):
         if relayed < lines - 1:
@@ -525,19 +533,14 @@
 
             @pl.when(i > 0)
             def _():
-                send_pair(functools.partial(send_x, c), i - 1)
-
-        send_x(c, partner_off, partner).start()
-        own_x(c).start()
-        if c == chunks - 1:
-            for s in range(1, subs):
-
-                @pl.loop(0, chips - 1)
-                def _(i):
-                    send_pair(functools.partial(send_x, c + s), i)
-
-                send_x(c + s, partner_off, partner).start()
-                own_x(c + s).start()
+                for u in now[c]:
+                    send_pair(functools.partial(send_x, u), i - 1)
+
+        for u in now[c]:
+            send_x(u, partner_off, partner).start()
+            own_x(u).start()
+        for u, steps in later[c]:
+            send_later(u, steps)
         if c == 0:
             keep_list.wait()
 
@@ -553,18 +556,17 @@
         relay(step)
     for step in range(1, lines):
         cross(step)
-    if share:
-        others(side_arrived)
+    others(side_arrived)
     keep_a.wait()
     move_table.wait()
     for at_z in range(lines):
-        for at_y in range(2):
-            at, sem = block(at_z, at_y, 1 - core), at_z * 2 + at_y
-            arrived(at, main, core_recv.at[sem], core_send.at[sem])
-            if share:
-                arrived(at, gets, core_side_recv.at[sem], core_side.at[sem])
+        for same in (True, False):
+            at, sem = block(at_z, y if same else 1 - y, 1 - core), place(at_z, same)[1]
+            arrived(at, main(same), core_recv.at[sem], core_send.at[sem])
+            if gets(same)[1]:
+                arrived(at, gets(same), core_side_recv.at[sem], core_side.at[sem])
     for s in range(subs):
-        for u in range(chunks) if s == 0 else [chunks - 1 + s]:
+        for u in range(s * chunks, (s + 1) * chunks):
             own_x(u).wait()
 
             @pl.loop(1, row_devices)
@@ -600,13 +602,12 @@
 
     for at_z in range(lines):
         over_y(at_z).wait_send()
-        for at_y in range(2):
-            over_core(at_z, at_y).wait_send()
-            if share:
-                side_core(at_z, at_y).wait_send()
-
-    if share:
-        others(lambda at_z, at_y: side_x(at_z, at_y).wait_send())
+        for same in (True, False):
+            over_core(at_z, same).wait_send()
+            if gets(same)[1]:
+                side_core(at_z, same).wait_send()
+
+    others(lambda at_z, same: side_x(at_z, same).wait_send())
     for c in range(chunks):
         for off in range(1, col_devices):
 
@@ -636,7 +637,7 @@
     slots, tile, _ = alpha_tiles.shape
     groups = alpha_rows.shape[1]
     chunks, strip = rows // width, columns // row_devices
-    part, units, lines = strip // subs, rows // width - 1 + subs, row_devices // 4
+    part, units, lines = strip // subs, rows // width * subs, row_devices // 4
     stored = slots * tile // width
     row_peers, col_peers = row_devices - 1, col_devices - 1
     dma, half = pltpu.SemaphoreType.DMA, jnp.bfloat16
@@ -681,7 +682,7 @@
             pltpu.SemaphoreType.REGULAR((lines,)),
         ],
         compiler_params=pltpu.CompilerParams(
-            collective_id=0, has_side_effects=True, vmem_limit_bytes=60 << 20
+            collective_id=0, has_side_effects=True, vmem_limit_bytes=48 << 20
         ),
         cost_estimate=pl.CostEstimate(flops=1 << 37, bytes_accessed=1 << 28, transcendentals=0),
         name="fused",

time: 145 us -> 141 us (0.972)
  Pallas kernels: 144 us -> 137 us
  local copies, waits for them, and re-layouts: 0 us -> 2.5 us
    pallas_call x1, Pallas kernels: 5.97 us -> 2.43 us  [final(): pl.pallas_call(functools.partial(final_kernel, block), in_specs=[whole] *...]
    pallas_call x1, Pallas kernels: 138 us -> 135 us  [fused(): pl.pallas_call(functools.partial(fused_kernel, chunks, subs, share), in_s...]
    unnamed x0 -> x8, local copies, waits for them, and re-layouts: none -> 2.5 us
where the time goes in v5:
time: 141 us; the launch traced here: 140 us
  Pallas kernels  137 us (97%)
  local copies, waits for them, and re-layouts  2.5 us (2%)
    pallas_call x1, Pallas kernels, fused(): pl.pallas_call(functools.partial(fused_kernel, chunks, subs, share), in_s...  135 us

profile of v5, /device:TPU:13, one launch (start us, length us, event | category | flops | bytes accessed | tf_op | source)
XLA Modules:
  0.0 139.9 jit_solution(2011764968082714737)
XLA Ops:
  0.0 0.0 copy-start.1
  0.0 1.1 copy-done.1
  1.1 0.0 copy-start.2
  1.1 0.7 copy-done.2
  1.8 0.0 copy-start.3
  1.8 0.7 copy-done.3
  2.5 0.0 copy-start
  2.5 134.9 %fused.1 = (bf16[16,192,384]{2,1,0:T(8,128)(2,1)S(1)}, bf16[2,192,3072]{2,1,0:T(8,128)(2,1)S(1)}) custom-call(s32[6,1,24]{2,1,0:T(1,128)S(1)} %bitcast.12, s32[1,2,1,4]{3,2,1,0:T(1,128)S(1)} %copy-done.3, bf16[384,3072]{1,0:T(8,128)(2,1)} %bitcast.14, bf16[24,768,128]{2,1,0:T(8,128)(2,1)} %bitcast.13, bf16[8,192,192]{2,1,0:T(8,128)(2,1)S(1)} %bitcast.11), custom_call_target="tpu_custom_call" | custom-call | flops 137438953472 | bytes 268435456 | tf_op jit(solution)/shard_map/fused/pallas_call | solution.py:646
  137.4 0.0 copy-done
  137.4 2.4 %final.1 = f32[384,3072]{1,0:T(8,128)} custom-call(bf16[3072,384]{1,0:T(8,128)(2,1)S(1)} %bitcast.9, bf16[384,3072]{1,0:T(8,128)(2,1)S(1)} %bitcast.10, f32[384,3072]{1,0:T(8,128)S(1)} %bitcast.8), custom_call_target="tpu_custom_call" | custom-call | tf_op jit(solution)/shard_map/final/pallas_call | solution.py:135
Async XLA Ops:
  0.0 1.1 copy-start.1
  1.1 0.7 copy-start.2
  1.8 0.7 copy-start.3
  2.5 134.9 %copy-start = (f32[2,192,3072]{2,1,0:T(8,128)S(1)}, f32[2,192,3072]{2,1,0:T(8,128)}, u32[]{:S(2)}) copy-start(f32[2,192,3072]{2,1,0:T(8,128)} %param.11) | copy-start | bytes 14155780

commit v6 on v5

--- a/solution.py
+++ b/solution.py
@@ -237,7 +237,7 @@
 
     def reach(i):
         odd = lax.rem(i, 2)
-        return chips // 2 + (1 - odd) * (i // 2) - odd * ((i + 1) // 2)
+        return lax.rem(i + 1, chips)
 
     def pair(i):
         return lax.rem(chip + reach(i), chips)
@@ -514,7 +514,7 @@
 
     load_b.wait()
     move_table = pltpu.make_async_copy(table, picks, t_sem)
-    now, later = [[0], [1], [2]], [[(3, straight)], [(3, turned), (4, straight)], [(5, straight), (4, turned), (5, turned)]]
+    now, later = [[0], [1], [2]], [[(3, straight), (3, turned)], [(4, straight)], [(5, straight), (4, turned), (5, turned)]]
     relayed = 0
     for c in range(chunks):
         if relayed < lines - 1:

time: 141 us -> 140 us (level)
  no operation moved by 1% of the time
where the time goes in v6:
time: 140 us
  Pallas kernels  137 us (98%)
  local copies, waits for them, and re-layouts  2.5 us (2%)
    pallas_call x1, Pallas kernels, fused(): pl.pallas_call(functools.partial(fused_kernel, chunks, subs, share), in_s...  135 us

profile of v6, /device:TPU:13, one launch (start us, length us, event | category | flops | bytes accessed | tf_op | source)
XLA Modules:
  0.0 140.0 jit_solution(8899255171555444331)
XLA Ops:
  0.0 0.0 copy-start.1
  0.0 1.1 copy-done.1
  1.1 0.0 copy-start.2
  1.1 0.7 copy-done.2
  1.8 0.0 copy-start.3
  1.8 0.7 copy-done.3
  2.5 0.0 copy-start
  2.5 135.1 %fused.1 = (bf16[16,192,384]{2,1,0:T(8,128)(2,1)S(1)}, bf16[2,192,3072]{2,1,0:T(8,128)(2,1)S(1)}) custom-call(s32[6,1,24]{2,1,0:T(1,128)S(1)} %bitcast.12, s32[1,2,1,4]{3,2,1,0:T(1,128)S(1)} %copy-done.3, bf16[384,3072]{1,0:T(8,128)(2,1)} %bitcast.14, bf16[24,768,128]{2,1,0:T(8,128)(2,1)} %bitcast.13, bf16[8,192,192]{2,1,0:T(8,128)(2,1)S(1)} %bitcast.11), custom_call_target="tpu_custom_call" | custom-call | flops 137438953472 | bytes 268435456 | tf_op jit(solution)/shard_map/fused/pallas_call | solution.py:646
  137.6 0.0 copy-done
  137.6 2.4 %final.1 = f32[384,3072]{1,0:T(8,128)} custom-call(bf16[3072,384]{1,0:T(8,128)(2,1)S(1)} %bitcast.9, bf16[384,3072]{1,0:T(8,128)(2,1)S(1)} %bitcast.10, f32[384,3072]{1,0:T(8,128)S(1)} %bitcast.8), custom_call_target="tpu_custom_call" | custom-call | tf_op jit(solution)/shard_map/final/pallas_call | solution.py:135
Async XLA Ops:
  0.0 1.1 copy-start.1
  1.1 0.7 copy-start.2
  1.8 0.7 copy-start.3
  2.5 135.1 %copy-start = (f32[2,192,3072]{2,1,0:T(8,128)S(1)}, f32[2,192,3072]{2,1,0:T(8,128)}, u32[]{:S(2)}) copy-start(f32[2,192,3072]{2,1,0:T(8,128)} %param.11) | copy-start | bytes 14155780

commit v7 on v6

--- a/solution.py
+++ b/solution.py
@@ -370,16 +370,26 @@
             over_y(z + 1 + step).start()
             spread(z + 1 + step, True)
 
-    def cross(step):
-        at_z = lax.rem(z + step, lines)
+    def at_distance(d, body):
+        @pl.when(z + d < lines)
+        def _():
+            body(z + d)
+
+        @pl.when(z >= d)
+        def _():
+            body(z - d)
+
+    def cross(at_z):
         arrived(block(at_z, 1 - y, core), main(False), y_recv.at[at_z], y_send.at[at_z])
         spread(at_z, False)
 
     def others(body):
-        for same, first in ((True, 1), (False, 0)):
-            if gives(same)[1]:
-                for step in range(first, lines):
-                    body(lax.rem(z + step, lines), same)
+        for d in range(lines):
+            for same in (True, False):
+                if gives(same)[1] and d > 0:
+                    at_distance(d, functools.partial(body, same=same))
+                elif gives(same)[1] and not same:
+                    body(z, same)
 
     def side_arrived(at_z, same):
         side_x(at_z, same).wait_recv()
@@ -550,12 +560,12 @@
 
             make_table()
             move_table.start()
-            cross(0)
+            cross(z)
 
     for step in range(relayed, lines - 1):
         relay(step)
-    for step in range(1, lines):
-        cross(step)
+    for d in range(1, lines):
+        at_distance(d, cross)
     others(side_arrived)
     keep_a.wait()
     move_table.wait()
@@ -621,14 +631,16 @@
         send_list(off).wait_send()
         for u in range(len(units)):
             send_x(u, off, peer).wait_send()
-        for s in range(subs):
-            send_own(s, off, peer).wait()
 
     for s in range(subs):
         stay_own(s).wait()
         stay_mirror(s).wait()
         for off in range(1, col_devices):
             send_mirror(s, off).wait()
+
+        @pl.loop(1, row_devices)
+        def _(off):
+            send_own(s, off, lax.rem(row + off, row_devices)).wait()
 
 
 def fused(c_matrix, beta_values, beta_rows, alpha_tiles, alpha_rows, row_devices, col_devices, subs, share):

time: 140 us -> 140 us (level)
  no operation moved by 1% of the time
where the time goes in v7:
time: 140 us
  Pallas kernels  137 us (98%)
  local copies, waits for them, and re-layouts  2.5 us (2%)
    pallas_call x1, Pallas kernels, fused(): pl.pallas_call(functools.partial(fused_kernel, chunks, subs, share), in_s...  135 us

profile of v7, /device:TPU:13, one launch (start us, length us, event | category | flops | bytes accessed | tf_op | source)
XLA Modules:
  0.0 139.9 jit_solution(18223543307801794578)
XLA Ops:
  0.0 0.0 copy-start.1
  0.0 1.1 copy-done.1
  1.1 0.0 copy-start.2
  1.1 0.7 copy-done.2
  1.8 0.0 copy-start.3
  1.8 0.7 copy-done.3
  2.5 0.0 copy-start
  2.5 135.0 %fused.1 = (bf16[16,192,384]{2,1,0:T(8,128)(2,1)S(1)}, bf16[2,192,3072]{2,1,0:T(8,128)(2,1)S(1)}) custom-call(s32[6,1,24]{2,1,0:T(1,128)S(1)} %bitcast.12, s32[1,2,1,4]{3,2,1,0:T(1,128)S(1)} %copy-done.3, bf16[384,3072]{1,0:T(8,128)(2,1)} %bitcast.14, bf16[24,768,128]{2,1,0:T(8,128)(2,1)} %bitcast.13, bf16[8,192,192]{2,1,0:T(8,128)(2,1)S(1)} %bitcast.11), custom_call_target="tpu_custom_call" | custom-call | flops 137438953472 | bytes 268435456 | tf_op jit(solution)/shard_map/fused/pallas_call | solution.py:658
  137.5 0.0 copy-done
  137.5 2.4 %final.1 = f32[384,3072]{1,0:T(8,128)} custom-call(bf16[3072,384]{1,0:T(8,128)(2,1)S(1)} %bitcast.9, bf16[384,3072]{1,0:T(8,128)(2,1)S(1)} %bitcast.10, f32[384,3072]{1,0:T(8,128)S(1)} %bitcast.8), custom_call_target="tpu_custom_call" | custom-call | tf_op jit(solution)/shard_map/final/pallas_call | solution.py:135
Async XLA Ops:
  0.0 1.1 copy-start.1
  1.1 0.7 copy-start.2
  1.8 0.7 copy-start.3
  2.5 135.0 %copy-start = (f32[2,192,3072]{2,1,0:T(8,128)S(1)}, f32[2,192,3072]{2,1,0:T(8,128)}, u32[]{:S(2)}) copy-start(f32[2,192,3072]{2,1,0:T(8,128)} %param.11) | copy-start | bytes 14155780

commit v8 on v7

--- a/solution.py
+++ b/solution.py
@@ -154,7 +154,7 @@
 
 def fused_kernel(chunks, subs, share, rows_ref, lists_ref, c_ref, b_ref, alpha_ref, own_ref, mirror_ref, *scratch):
     held, sent, xt = scratch[:chunks], scratch[chunks : 2 * chunks], scratch[2 * chunks : 2 * chunks + subs]
-    (b_own, flat, a_own, a_all, xr, stack, own_out, mirror_out, list_own, list_all, table, picks,
+    (b_own, a_own, a_all, xr, stack, own_out, mirror_out, list_own, list_all, table, picks,
      load_sem, c_own, c_send, c_recv, x_own, x_send, x_recv, l_own, l_send, l_recv, a_sem,
      up_send, up_recv, down_send, down_recv, y_send, y_recv, core_send, core_recv,
      x_side, x_side_recv, core_side, core_side_recv, t_sem,
@@ -164,7 +164,7 @@
     rows, columns = c_ref.shape
     tiles, depth, width = b_own.shape
     listed_b = depth // width
-    slots, tile, _ = flat.shape
+    slots, tile, _ = alpha_ref.shape
     groups = lists_ref.shape[1]
     listed = slots // groups
     chunk, strip = rows // chunks, columns // row_devices
@@ -467,8 +467,6 @@
             mirror_out[s, g, :, pl.ds(start, 2 * tile)] = jnp.concatenate(found[g], axis=1)
 
     load_b = pltpu.make_async_copy(b_ref, b_own, load_sem.at[0])
-    load_a = pltpu.make_async_copy(alpha_ref, flat, load_sem.at[1])
-    load_a.start()
     barrier = pltpu.get_barrier_semaphore()
     signal_near(barrier)
     lane = lax.broadcasted_iota(jnp.int32, list_own.shape, 1)
@@ -477,9 +475,8 @@
         for s in range(listed):
             mine = jnp.where(lane == row * slots + g * listed + s, lists_ref[0, g, 0, s], mine)
     list_own[...] = mine
-    load_a.wait()
     for s in range(listed):
-        first, second = flat[s], flat[listed + s]
+        first, second = alpha_ref[s], alpha_ref[listed + s]
         a_own[s] = first[:, :width]
         a_own[listed + s] = second[:, tile - width :]
         a_own[slots + s] = jnp.concatenate([first[:, width:], second[:, : tile - width]], axis=1)
@@ -657,7 +654,7 @@
     scalars = pl.BlockSpec(memory_space=pltpu.SMEM)
     return pl.pallas_call(
         functools.partial(fused_kernel, chunks, subs, share),
-        in_specs=[scalars, scalars, anywhere, anywhere, anywhere],
+        in_specs=[scalars, scalars, anywhere, anywhere, pl.BlockSpec(memory_space=pltpu.VMEM)],
         out_specs=[anywhere, anywhere],
         out_shape=[
             jax.ShapeDtypeStruct((row_devices, strip, groups * tile), half),
@@ -668,7 +665,6 @@
         + [pltpu.VMEM((row_devices * groups, part, 2 * width), half)] * subs
         + [
             pltpu.VMEM((tiles, listed * width, width), half),
-            pltpu.VMEM((slots, tile, tile), half),
             pltpu.VMEM((stored, tile, width), half),
             pltpu.VMEM((row_devices * stored, tile, width), half),
             pltpu.VMEM((chunks, row_devices, strip, width), half),
@@ -679,7 +675,7 @@
             pltpu.VMEM((row_devices, 8, width), jnp.int32),
             pltpu.VMEM((8, width), jnp.int32),
             pltpu.SMEM((8, width), jnp.int32),
-            dma((2,)),
+            dma((1,)),
             dma((chunks, tiles)), dma((chunks, col_peers, tiles)), dma((chunks, col_peers, tiles)),
             dma((units,)), dma((units, row_peers)), dma((units, row_peers)),
             dma, dma((row_peers,)), dma((row_peers,)), dma,

time: 140 us -> 140 us (level)
  no operation moved by 1% of the time
where the time goes in v8:
time: 140 us
  Pallas kernels  137 us (98%)
  local copies, waits for them, and re-layouts  2.5 us (2%)
    pallas_call x1, Pallas kernels, fused(): pl.pallas_call(functools.partial(fused_kernel, chunks, subs, share), in_s...  135 us

profile of v8, /device:TPU:13, one launch (start us, length us, event | category | flops | bytes accessed | tf_op | source)
XLA Modules:
  0.0 139.8 jit_solution(2684561471880403780)
XLA Ops:
  0.0 0.0 copy-start.1
  0.0 1.1 copy-done.1
  1.1 0.0 copy-start.2
  1.1 0.7 copy-done.2
  1.8 0.0 copy-start.3
  1.8 0.7 copy-done.3
  2.5 0.0 copy-start
  2.5 134.9 %fused.1 = (bf16[16,192,384]{2,1,0:T(8,128)(2,1)S(1)}, bf16[2,192,3072]{2,1,0:T(8,128)(2,1)S(1)}) custom-call(s32[6,1,24]{2,1,0:T(1,128)S(1)} %bitcast.12, s32[1,2,1,4]{3,2,1,0:T(1,128)S(1)} %copy-done.3, bf16[384,3072]{1,0:T(8,128)(2,1)} %bitcast.14, bf16[24,768,128]{2,1,0:T(8,128)(2,1)} %bitcast.13, bf16[8,192,192]{2,1,0:T(8,128)(2,1)S(1)} %bitcast.11), custom_call_target="tpu_custom_call" | custom-call | flops 137438953472 | bytes 268435456 | tf_op jit(solution)/shard_map/fused/pallas_call | solution.py:655
  137.4 0.0 copy-done
  137.4 2.4 %final.1 = f32[384,3072]{1,0:T(8,128)} custom-call(bf16[3072,384]{1,0:T(8,128)(2,1)S(1)} %bitcast.9, bf16[384,3072]{1,0:T(8,128)(2,1)S(1)} %bitcast.10, f32[384,3072]{1,0:T(8,128)S(1)} %bitcast.8), custom_call_target="tpu_custom_call" | custom-call | tf_op jit(solution)/shard_map/final/pallas_call | solution.py:135
Async XLA Ops:
  0.0 1.1 copy-start.1
  1.1 0.7 copy-start.2
  1.8 0.7 copy-start.3
  2.5 134.9 %copy-start = (f32[2,192,3072]{2,1,0:T(8,128)S(1)}, f32[2,192,3072]{2,1,0:T(8,128)}, u32[]{:S(2)}) copy-start(f32[2,192,3072]{2,1,0:T(8,128)} %param.11) | copy-start | bytes 14155780

commit v9 on v8

--- a/solution.py
+++ b/solution.py
@@ -456,7 +456,7 @@
             stack[p] = run.astype(stack.dtype)
             return run
 
-        lax.fori_loop(0, width, step, jnp.zeros((part, tile), jnp.float32), unroll=16)
+        lax.fori_loop(0, width, step, jnp.zeros((part, tile), jnp.float32), unroll=32)
 
     def assemble(s, k):
         found = [[stack[picks[4, g * row_devices + 2 * k + e]] for e in range(2)] for g in range(groups)]

time: 140 us -> 140 us (level)
  no operation moved by 1% of the time
where the time goes in v9:
time: 140 us
  Pallas kernels  137 us (98%)
  local copies, waits for them, and re-layouts  2.5 us (2%)
    pallas_call x1, Pallas kernels, fused(): pl.pallas_call(functools.partial(fused_kernel, chunks, subs, share), in_s...  135 us

profile of v9, /device:TPU:13, one launch (start us, length us, event | category | flops | bytes accessed | tf_op | source)
XLA Modules:
  0.0 139.8 jit_solution(721997996805100620)
XLA Ops:
  0.0 0.0 copy-start.1
  0.0 1.1 copy-done.1
  1.1 0.0 copy-start.2
  1.1 0.7 copy-done.2
  1.8 0.0 copy-start.3
  1.8 0.7 copy-done.3
  2.5 0.0 copy-start
  2.5 134.9 %fused.1 = (bf16[16,192,384]{2,1,0:T(8,128)(2,1)S(1)}, bf16[2,192,3072]{2,1,0:T(8,128)(2,1)S(1)}) custom-call(s32[6,1,24]{2,1,0:T(1,128)S(1)} %bitcast.12, s32[1,2,1,4]{3,2,1,0:T(1,128)S(1)} %copy-done.3, bf16[384,3072]{1,0:T(8,128)(2,1)} %bitcast.14, bf16[24,768,128]{2,1,0:T(8,128)(2,1)} %bitcast.13, bf16[8,192,192]{2,1,0:T(8,128)(2,1)S(1)} %bitcast.11), custom_call_target="tpu_custom_call" | custom-call | flops 137438953472 | bytes 268435456 | tf_op jit(solution)/shard_map/fused/pallas_call | solution.py:655
  137.4 0.0 copy-done
  137.4 2.4 %final.1 = f32[384,3072]{1,0:T(8,128)} custom-call(bf16[3072,384]{1,0:T(8,128)(2,1)S(1)} %bitcast.9, bf16[384,3072]{1,0:T(8,128)(2,1)S(1)} %bitcast.10, f32[384,3072]{1,0:T(8,128)S(1)} %bitcast.8), custom_call_target="tpu_custom_call" | custom-call | tf_op jit(solution)/shard_map/final/pallas_call | solution.py:135
Async XLA Ops:
  0.0 1.1 copy-start.1
  1.1 0.7 copy-start.2
  1.8 0.7 copy-start.3
  2.5 134.9 %copy-start = (f32[2,192,3072]{2,1,0:T(8,128)S(1)}, f32[2,192,3072]{2,1,0:T(8,128)}, u32[]{:S(2)}) copy-start(f32[2,192,3072]{2,1,0:T(8,128)} %param.11) | copy-start | bytes 14155780
